TPU v7x, 128 devices: a whole 4x4x4 slice. The times are simulated.
128 devices in a mesh: req: 4 (over z_lo, core), seq: 32 (over y, x, z_hi).
Axes of the slice: x: 4, y: 4, z: 4 (z_hi: 2, z_lo: 2; z = z_hi * 2 + z_lo), core: 2. Of those that a mesh axis runs over, the one named last changes fastest.
Arguments:
- prefill_query: bfloat16 [16384, 1536], P(('req', 'seq')), may hold values from -512 to 512
- prefill_key: bfloat16 [16384, 512], P(('req', 'seq')), may hold values from -512 to 512
- prefill_value: bfloat16 [16384, 512], P(('req', 'seq')), may hold values from -6 to 6
- prefill_resid: bfloat16 [16384, 1536], P(('req', 'seq')), may hold values from -6 to 6
- dec_query: bfloat16 [16, 1536], P('req'), may hold values from -512 to 512
- dec_key_new: bfloat16 [16, 512], P('req'), may hold values from -16 to 16
- dec_value_new: bfloat16 [16, 512], P('req'), may hold values from -6 to 6
- dec_resid: bfloat16 [16, 1536], P('req'), may hold values from -6 to 6
- cache_lengths: int32 [16], P('req'), may hold values from 16 to 32768, as said below
- key_cache: bfloat16 [16, 32768, 512], P('req', 'seq'), may hold values from -512 to 512
- value_cache: bfloat16 [16, 32768, 512], P('req', 'seq'), may hold values from -6 to 6
- attn_out_weight: bfloat16 [1536, 1536], replicated, may hold values from -0.15625 to 0.15625
- ffn_gain: float32 [1536], replicated, may hold values from 0.1 to 1.9
- expert_gate: bfloat16 [32, 1536, 512], P('seq', 'req'), may hold values from -0.15625 to 0.15625
- expert_up: bfloat16 [32, 1536, 512], P('seq', 'req'), may hold values from -0.15625 to 0.15625
- expert_down: bfloat16 [32, 512, 1536], P('seq', None, 'req'), may hold values from -0.25 to 0.25
- routes: int32 [16384, 8], P(('req', 'seq')), may hold values from 0 to 31, all different within a row; in each aligned block of 128 rows (0 to 127, 128 to 255, ...) at most 40 rows name the same one
- route_weights: float32 [16384, 8], P(('req', 'seq')), may hold values from 0.05 to 0.5
Outputs:
- prefill_out: bfloat16 [16384, 1536], P(('req', 'seq'))
- dec_out: bfloat16 [16, 1536], P('req')
Inputs may be any that keep to these rules, and one draw needn't show every extreme that they name: `routes`: in each aligned block of 128 rows (the rows of one device) no expert is named by more than 40 rows. `cache_lengths`: some request uses all 32768 positions.
All inputs are finite; a program needn't handle non-finite values.
Results may differ from a plain program's by a relative error of at most 0.012.
Values may be sent and summed in bfloat16 or wider, within the bound.
No kernel may reach another device: no remote copies, remote signals or barrier semaphores. Data moves between devices by JAX's collectives and lax.ppermute only.
A program may use at most 128 MiB of HBM per device.

v0:
```python
import math

import jax
import jax.numpy as jnp
from jax import lax
from jax.sharding import PartitionSpec as P

D = 1536
HEADS = 24
KVH = 8
HD = 64
EXPERTS = 32
CAP = 40


NEGATIVE = -1e30
EPSILON = 1e-05


def rms_scale(hidden, gain):
    values_float = hidden.astype(jnp.float32)
    mean_square = jnp.mean(values_float * values_float, axis=-1, keepdims=True)
    return (values_float * lax.rsqrt(mean_square + EPSILON) * gain).astype(jnp.bfloat16)


def per_request(function, operands):
    return jax.vmap(function)(operands)


def prefill_attention(prefill_query, prefill_key, prefill_value):
    token_rows = prefill_query.shape[0]
    group_size = HEADS // KVH
    score_scale = 1.0 / math.sqrt(HD)
    own_start = lax.axis_index("seq") * token_rows
    query_position = own_start + jnp.arange(token_rows, dtype=jnp.int32)
    query_heads = prefill_query.reshape(token_rows, KVH, group_size, HD)
    initial = (
        jnp.full((KVH, group_size, token_rows), NEGATIVE, jnp.float32),
        jnp.zeros((KVH, group_size, token_rows), jnp.float32),
        jnp.zeros((token_rows, KVH, group_size, HD), jnp.float32),
    )
    key_rows = lax.all_gather(prefill_key, "seq", axis=0, tiled=True)
    value_rows = lax.all_gather(prefill_value, "seq", axis=0, tiled=True)
    key_count = key_rows.shape[0]
    block_rows = 512
    key_heads = key_rows.reshape(key_count, KVH, HD)
    value_heads = value_rows.reshape(key_count, KVH, HD)

    def add_block(number, running_state):
        maxima, totals, weighted = running_state
        offset = number * block_rows
        key_block = lax.dynamic_slice_in_dim(key_heads, offset, block_rows, 0)
        value_block = lax.dynamic_slice_in_dim(value_heads, offset, block_rows, 0)
        key_position = offset + jnp.arange(block_rows, dtype=jnp.int32)
        visible = (key_position[None, :] <= query_position[:, None])[None, None, :, :]
        logits = (
            jnp.einsum("qkgd,pkd->kgqp", query_heads, key_block, preferred_element_type=jnp.float32)
            * score_scale
        )
        logits = jnp.where(visible, logits, NEGATIVE)
        new_maxima = jnp.maximum(maxima, jnp.max(logits, axis=-1))
        exponent = jnp.where(visible, jnp.exp(logits - new_maxima[..., None]), 0.0)
        rescale = jnp.exp(maxima - new_maxima)
        totals = totals * rescale + jnp.sum(exponent, axis=-1)
        weighted = weighted * jnp.moveaxis(rescale, 2, 0)[..., None] + jnp.einsum(
            "kgqp,pkd->qkgd",
            exponent.astype(jnp.bfloat16),
            value_block,
            preferred_element_type=jnp.float32,
        )
        return (new_maxima, totals, weighted)

    maxima, totals, weighted = lax.fori_loop(0, key_count // block_rows, add_block, initial)
    return (
        (weighted / jnp.moveaxis(totals, 2, 0)[..., None])
        .reshape(token_rows, HEADS * HD)
        .astype(jnp.bfloat16)
    )


def decode_attention(dec_query, dec_key_new, dec_value_new, cache_lengths, key_cache, value_cache):
    requests, block_length, feature_width = key_cache.shape
    group_size = HEADS // KVH
    score_scale = 1.0 / math.sqrt(HD)
    first_position = lax.axis_index("seq") * block_length
    positions = first_position + jnp.arange(block_length, dtype=jnp.int32)
    valid_mask = positions[None, :] < cache_lengths[:, None]
    query_heads = dec_query.reshape(requests, KVH, group_size, HD)
    key_heads = key_cache.reshape(requests, block_length, KVH, HD)
    value_heads = value_cache.reshape(requests, block_length, KVH, HD)

    def scores_of(pieces):
        query_one, keys_one, valid_one = pieces
        logits = (
            jnp.einsum("kgd,pkd->kgp", query_one, keys_one, preferred_element_type=jnp.float32)
            * score_scale
        )
        return jnp.where(valid_one[None, None, :], logits, NEGATIVE)

    def terms_of(pieces):
        scores_one, maxima_one, values_one, valid_one = pieces
        exponent = jnp.where(
            valid_one[None, None, :], jnp.exp(scores_one - maxima_one[..., None]), 0.0
        )
        weighted_one = jnp.einsum(
            "kgp,pkd->kgd",
            exponent.astype(jnp.bfloat16),
            values_one,
            preferred_element_type=jnp.float32,
        )
        return (jnp.sum(exponent, axis=-1), weighted_one)

    scores = per_request(scores_of, (query_heads, key_heads, valid_mask))
    local_maxima = jnp.max(scores, axis=-1)
    maxima = lax.pmax(local_maxima, "seq")
    totals, weighted = per_request(terms_of, (scores, maxima, value_heads, valid_mask))
    totals, weighted = lax.psum((totals, weighted), "seq")
    fresh_score = (
        jnp.einsum(
            "rkgd,rkd->rkg",
            query_heads,
            dec_key_new.reshape(requests, KVH, HD),
            preferred_element_type=jnp.float32,
        )
        * score_scale
    )
    final_maxima = jnp.maximum(maxima, fresh_score)
    rescale = jnp.exp(maxima - final_maxima)
    fresh_exp = jnp.exp(fresh_score - final_maxima)
    denominator = totals * rescale + fresh_exp
    fresh_weight = lax.optimization_barrier(fresh_exp.astype(jnp.bfloat16)).astype(jnp.float32)
    numerator = weighted * rescale[..., None] + fresh_weight[..., None] * dec_value_new.reshape(
        requests, KVH, 1, HD
    ).astype(jnp.float32)
    return (numerator / denominator[..., None]).reshape(requests, HEADS * HD).astype(jnp.bfloat16)


def expert_rows(rows_batch, gate_full, up_full, down_full):
    gate_value = jnp.einsum(
        "erd,edf->erf", rows_batch, gate_full, preferred_element_type=jnp.float32
    )
    up_value = jnp.einsum("erd,edf->erf", rows_batch, up_full, preferred_element_type=jnp.float32)
    hidden = (jax.nn.silu(gate_value) * up_value).astype(jnp.bfloat16)
    return jnp.einsum("erf,efd->erd", hidden, down_full, preferred_element_type=jnp.float32).astype(
        jnp.bfloat16
    )


def body(
    prefill_query,
    prefill_key,
    prefill_value,
    prefill_resid,
    dec_query,
    dec_key_new,
    dec_value_new,
    dec_resid,
    cache_lengths,
    key_cache,
    value_cache,
    attn_out_weight,
    ffn_gain,
    expert_gate,
    expert_up,
    expert_down,
    routes,
    route_weights,
):
    attended = prefill_attention(prefill_query, prefill_key, prefill_value)
    middle = (
        prefill_resid.astype(jnp.float32)
        + jnp.dot(attended, attn_out_weight, preferred_element_type=jnp.float32)
    ).astype(jnp.bfloat16)
    normed = rms_scale(middle, ffn_gain)
    gate_full, up_full = (
        lax.all_gather(expert_gate, "req", axis=1, tiled=True),
        lax.all_gather(expert_up, "req", axis=1, tiled=True),
    )
    down_full = lax.all_gather(expert_down, "req", axis=2, tiled=True)
    token_rows, top_count = routes.shape
    flat_expert = routes.reshape(-1)
    token_index = jnp.arange(token_rows * top_count, dtype=jnp.int32) // top_count
    onehot = (flat_expert[:, None] == jnp.arange(EXPERTS, dtype=jnp.int32)[None, :]).astype(
        jnp.int32
    )
    earlier = jnp.cumsum(onehot, axis=0) - onehot
    slot_index = jnp.sum(earlier * onehot, axis=1)
    outgoing = (
        jnp.zeros((EXPERTS, CAP, D), jnp.bfloat16)
        .at[flat_expert, slot_index]
        .set(normed[token_index])
    )
    incoming = lax.all_to_all(outgoing[:, None], "seq", split_axis=0, concat_axis=1, tiled=True)
    local_experts, sources, slot_count, feature_width = incoming.shape
    result = expert_rows(
        incoming.reshape(local_experts, sources * slot_count, feature_width),
        gate_full,
        up_full,
        down_full,
    )
    result = result.reshape(local_experts, sources, slot_count, feature_width)
    returned = lax.all_to_all(result, "seq", split_axis=1, concat_axis=0, tiled=True)
    picked = returned.reshape(EXPERTS, CAP, D)[flat_expert, slot_index]
    picked = picked.reshape(token_rows, top_count, D)
    mixture = jnp.sum(route_weights[..., None] * picked.astype(jnp.float32), axis=1)
    prefill_out = (middle.astype(jnp.float32) + mixture).astype(jnp.bfloat16)
    decoded = decode_attention(
        dec_query, dec_key_new, dec_value_new, cache_lengths, key_cache, value_cache
    )
    dec_out = (
        dec_resid.astype(jnp.float32)
        + jnp.dot(decoded, attn_out_weight, preferred_element_type=jnp.float32)
    ).astype(jnp.bfloat16)
    return (prefill_out, dec_out)


def solution(mesh):
    return jax.shard_map(
        body,
        mesh=mesh,
        in_specs=(
            P(("req", "seq"), None),
            P(("req", "seq"), None),
            P(("req", "seq"), None),
            P(("req", "seq"), None),
            P("req", None),
            P("req", None),
            P("req", None),
            P("req", None),
            P("req"),
            P("req", "seq", None),
            P("req", "seq", None),
            P(),
            P(),
            P("seq", "req", None),
            P("seq", "req", None),
            P("seq", None, "req"),
            P(("req", "seq"), None),
            P(("req", "seq"), None),
        ),
        out_specs=(P(("req", "seq"), None), P("req", None)),
        check_vma=False,
    )
```

profile of v0, /device:TPU:0, one launch (start us, length us, event | category | flops | bytes accessed | tf_op | source)
XLA Modules:
  0.0 821.3 jit_solution(3442623777327935929)
XLA Ops:
  11.1 1.2 copy.41
  12.3 9.0 %reduce-window.6 = s32[32,8,128]{2,1,0:T(8,128)S(1)} reduce-window(s32[32,8,128]{2,1,0:T(8,128)S(1)} %fusion.51, s32[]{:T(128)} %constant.93.clone.1), window={size=1x1x128 pad=0_0x0_0x127_0}, to_apply=%region_4.5 | reduce-window | flops 4161536 | bytes 262148 | tf_op jit(solution)/shard_map/reduce-window
  23.4 72.7 %all-gather.6.cloned.1.call-done = bf16[4096,512]{1,0:T(8,128)(2,1)} async-done(((bf16[128,512]{1,0:T(8,128)(2,1)}), bf16[4096,512]{1,0:T(8,128)(2,1)}) %all-gather.6.cloned.1.call-update) | async-done | bytes 4194320 | tf_op jit(solution)/shard_map/all_gather | solution.py:42
  96.1 6.4 copy.40
  102.5 75.9 %all-gather.8.cloned.1.call-done = bf16[4096,512]{1,0:T(8,128)(2,1)} async-done(((bf16[128,512]{1,0:T(8,128)(2,1)}), bf16[4096,512]{1,0:T(8,128)(2,1)}) %all-gather.8.cloned.1.call-update) | async-done | bytes 4194320 | tf_op jit(solution)/shard_map/all_gather | solution.py:43
  178.4 6.4 copy.42
  184.8 98.8 %while.18 = (s32[]{:T(128)}, f32[8,3,128]{2,1,0:T(4,128)S(1)}, f32[8,3,128]{2,1,0:T(4,128)S(1)}, f32[128,8,3,64]{0,3,2,1:T(8,128)S(1)}, bf16[4096,8,64]{0,2,1:T(...) while((s32[]{:T(128)}, f32[8,3,128]{2,1,0:T(4,128)S(1)}, ...), condition=%wide.region_3.4_spmd.clone, body=%wide.region_0.3_spmd.clone.sunk | while | flops 423774848 | bytes 47518944 | solution.py:73
  185.0 4.8 fusion.83
  189.8 4.5 fusion.85
  194.5 2.8 fusion.87
  197.5 4.8 fusion.83
  202.3 4.4 fusion.85
  206.9 2.8 fusion.87
  209.8 4.8 fusion.83
  214.6 4.4 fusion.85
  219.2 2.8 fusion.87
  222.2 4.8 fusion.83
  227.0 4.4 fusion.85
  231.6 2.8 fusion.87
  234.5 4.8 fusion.83
  239.3 4.4 fusion.85
  243.9 2.8 fusion.87
  246.8 4.8 fusion.83
  251.6 4.4 fusion.85
  256.2 2.8 fusion.87
  259.2 4.8 fusion.83
  263.9 4.4 fusion.85
  268.5 2.8 fusion.87
  271.5 4.8 fusion.83
  276.3 4.4 fusion.85
  280.8 2.8 fusion.87
  283.7 3.2 multiply_reduce_fusion
  287.0 0.9 copy-done.1
  288.0 18.6 %scatter_custom_fusion = bf16[1280,1536]{1,0:T(8,128)(2,1)} fusion(s32[1024]{0:T(1024)S(1)} %get-tuple-element.207, bf16[128,1536]{1,0:T(8,128)(2,1)S(1)} %multiply_convert_fusion, s32[1024]{0:T(1024)S(1)} %get-tuple-element.206, bf16[]{:T(256)} %constant.98.clone.1), kind=kCustom, calls=%fused_computation.36 | custom fusion | bytes 3932162
  306.7 5.1 all-to-all-start
  312.4 52.8 %all-to-all-done = bf16[32,1,40,1536]{3,2,1,0:T(8,128)(2,1)} async-done(((bf16[32,1,40,1536]{3,2,1,0:T(8,128)(2,1)}), bf16[32,1,40,1536]{3,2,1,0:T(8,128)(2,1)}, u32[]{:S(2)}, u32[]{:S(2)}) %all-to-all-start) | async-done | bytes 3932192 | tf_op jit(solution)/shard_map/all_to_all | solution.py:193
  365.2 4.8 fusion.36
  370.1 9.5 %convolution_convert_fusion = bf16[1280,1536]{1,0:T(8,128)(2,1)} fusion(bf16[1,512,1536]{2,1,0:T(8,128)(2,1)} %all-gather.14.cloned.1.call-done, bf16[1280,1536]{1,0:T(8,128)(2,1)} %bitcast.10, f32[1280,512]{1,0:T(8,128)S(1)} %fusion.36, bf16[1,1536,512]{2,1,0:T(8,128)(2,1)} %all-gather.12.cloned.1.call-done), kind=kOutput, calls=%fused_computation.32 | convolution fusion | flops 4032430080 | bytes 13631488 | tf_op jit(solution)/shard_map/erf,efd->erd/dot_general | solution.py:144
  379.5 7.5 all-to-all-start.1
  387.2 6.3 copy.51
  393.7 6.3 copy.50
  400.2 2.9 fusion.58
  403.2 205.7 %pmax.7 = f32[4,8,3]{2,1,0:T(8,128)S(1)} all-reduce(f32[4,8,3]{2,1,0:T(8,128)S(1)} %get-tuple-element.204), channel_id=1, replica_groups=mesh['req'=4,'seq'=32] {'seq'}, use_global_device_ids=true, to_apply=%region_11.12 | all-reduce | flops 96 | bytes 768 | tf_op jit(solution)/shard_map/pmax | solution.py:115
  609.3 3.5 fusion.43
  612.7 176.5 %all-reduce = (f32[4,8,3,64]{3,2,1,0:T(4,128)S(1)}, f32[4,8,3]{2,1,0:T(8,128)S(1)}) all-reduce(f32[4,8,3,64]{3,2,1,0:T(4,128)S(1)} %fusion.43, f32[4,8,3]{2,1,0:T(8,128)S(1)} %fusion.41), channel_id=1, replica_groups=mesh['req'=4,'seq'=32] {'seq'}, use_global_device_ids=true, to_apply=%region_12.13 | all-reduce | flops 6240 | bytes 49920 | tf_op jit(solution)/shard_map/psum | solution.py:117
  789.7 3.7 fusion.32
  793.4 17.8 %gather_fusion = bf16[1024,1536]{1,0:T(8,128)(2,1)S(1)} fusion(bf16[32,40,1536]{2,1,0:T(8,128)(2,1)} %bitcast.16, s32[1024]{0:T(1024)S(1)} %bitcast.111), kind=kCustom, calls=%fused_computation.1 | custom fusion | bytes 6299648 | tf_op jit(solution)/shard_map/gather | solution.py:203
  811.2 2.8 fusion.26
  (133 shorter events, 11.4 us)
Async XLA Ops:
  7.2 88.9 %all-gather.6.cloned.1.call-start = ((), (), s32[]{:S(2)}) async-start(), calls=%async_computation.2 | async-start | bytes 4325376 | tf_op jit(solution)/shard_map/all_gather | solution.py:42
  7.9 170.5 %all-gather.8.cloned.1.call-start = ((), (), s32[]{:S(2)}) async-start(), calls=%async_computation.3 | async-start | bytes 4325376 | tf_op jit(solution)/shard_map/all_gather | solution.py:43
  8.6 303.7 %all-gather.10.cloned.1.call-start = ((), (), s32[]{:S(2)}) async-start(), calls=%async_computation.4 | async-start | bytes 1966080 | tf_op jit(solution)/shard_map/all_gather | solution.py:176
  9.4 360.7 %all-gather.14.cloned.1.call-start = ((), (), s32[]{:S(2)}) async-start(), calls=%async_computation.6 | async-start | bytes 1966080 | tf_op jit(solution)/shard_map/all_gather | solution.py:179
  184.8 98.9 %copy-start.3 = (bf16[128,1536]{1,0:T(8,128)(2,1)S(1)}, bf16[128,1536]{1,0:T(8,128)(2,1)}, u32[]{:S(2)}) copy-start(bf16[128,1536]{1,0:T(8,128)(2,1)} %param.23) | copy-start | bytes 1179652
  189.8 4.7 copy-start
  202.3 4.6 copy-start
  214.6 4.6 copy-start
  227.0 4.6 copy-start
  239.3 4.6 copy-start
  251.6 4.6 copy-start
  263.9 4.6 copy-start
  276.2 4.6 copy-start
  283.6 4.3 copy-start.6
  287.0 0.9 copy-start.1
  306.7 58.5 %all-to-all-start = ((bf16[32,1,40,1536]{3,2,1,0:T(8,128)(2,1)}), bf16[32,1,40,1536]{3,2,1,0:T(8,128)(2,1)}, u32[]{:S(2)}, u32[]{:S(2)}) async-start(bf16[32,1,40,1536]{3,2,1,0:T(8,128)(2,1)} %bitcast.114), calls=%async_computation | async-start | bytes 7864320 | tf_op jit(solution)/shard_map/all_to_all | solution.py:193
  311.8 58.3 %all-gather.12.cloned.1.call-start = ((), (), s32[]{:S(2)}) async-start(), calls=%async_computation.5 | async-start | bytes 1966080 | tf_op jit(solution)/shard_map/all_gather | solution.py:177
  379.5 7.6 copy-start.7
  379.5 413.8 %all-to-all-start.1 = ((bf16[1,32,40,1536]{3,2,0,1:T(8,128)(2,1)}), bf16[1,32,40,1536]{3,2,0,1:T(8,128)(2,1)}, u32[]{:S(2)}, u32[]{:S(2)}) async-start(bf16[1,32,40,1536]{3,2,0,1:T(8,128)(2,1)} %bitcast.118), calls=%async_computation.1 | async-start | bytes 7864320 | tf_op jit(solution)/shard_map/all_to_all | solution.py:202
  387.2 6.3 copy-start.4
  393.6 6.4 copy-start.8
  393.6 6.4 copy-start.9
  393.7 6.5 copy-start.10
  403.2 386.5 %copy-start.5 = (bf16[4,1536]{1,0:T(4,128)(2,1)S(1)}, bf16[4,1536]{1,0:T(4,128)(2,1)}, u32[]{:S(2)}) copy-start(bf16[4,1536]{1,0:T(4,128)(2,1)} %param.27) | copy-start | bytes 36868
  811.2 2.8 copy-start.2
Sparse Core Ops, SparseCore 0:
  11.0 85.0 all-gather.5
  99.1 79.3 all-gather.7
  180.1 21.5 all-gather.9
  203.2 25.7 all-gather.13
  313.9 54.2 all-gather.11
where the time goes:
time: 823 us; the launch traced here: 821 us
  blocking collectives  382 us (46%)
  waiting for transfers between devices  204 us (25%)
  matrix products  88 us (11%)
  local copies, waits for them, and re-layouts  67.1 us (8%)
  other arithmetic  52 us (6%)
  between operations  14.1 us (2%)
  starting transfers between devices  13 us (2%)
    pmax x1, blocking collectives, decode_attention(): maxima = lax.pmax(local_maxima, 'seq')  206 us
    psum x1, blocking collectives, decode_attention(): totals, weighted = lax.psum((totals, weighted), 'seq')  176 us
    all_gather x1, waiting for transfers between devices, prefill_attention(): value_rows = lax.all_gather(prefill_value, 'seq', axis=0, tiled=True)  75.9 us
    all_gather x1, waiting for transfers between devices, prefill_attention(): key_rows = lax.all_gather(prefill_key, 'seq', axis=0, tiled=True)  72.7 us
    all_to_all x1, waiting for transfers between devices, body(): lax.all_to_all(outgoing[:, None], 'seq', split_axis=0, concat_axis=1, til...  52.8 us
    dot_general x8, matrix products, add_block(): jnp.einsum('qkgd,pkd->kgqp', query_heads, key_block, preferred_element_ty...  38.2 us
    reduce_sum x8, other arithmetic, add_block(): totals = totals * rescale + jnp.sum(exponent, axis=-1)  35.4 us
    unnamed x26, local copies, waits for them, and re-layouts  34.3 us
  transfers between devices with their start and end apart: 7, of which 3 were waited for; matrix products, arithmetic and copies ran while one was open for 21% of the time, Pallas kernels for 0%

commit v1 on v0

v1 whole, which is shorter than its diff:
```python
import jax
import jax.numpy as jnp
from jax import lax
from jax.experimental import pallas as pl
from jax.experimental.pallas import tpu as pltpu
from jax.sharding import PartitionSpec as P

D = 1536
HEADS = 24
KVH = 8
GROUP = HEADS // KVH
HD = 64
FFE = 512
EXPERTS = 32
CAP = 40
TOK = 128
SEQ = 32
PARTS = SEQ // KVH
STRIP = TOK // PARTS
HALF = STRIP // 2
QROWS = GROUP * HALF
PACK = TOK + QROWS
SLOTS = EXPERTS * CAP
CBLK = 1024
RLOC = 4

NEGATIVE = -1e30
EPSILON = 1e-05
SCALE = 0.125
F32 = jnp.float32
BF16 = jnp.bfloat16
MIB = 1 << 20


def swap_halves(x):
    return jnp.concatenate([x[..., HD:], x[..., :HD]], axis=-1)


def left_lanes(shape):
    return lax.broadcasted_iota(jnp.int32, shape, len(shape) - 1) < HD


def dot_nt(a, b):
    return lax.dot_general(a, b, (((1,), (1,)), ((), ())), preferred_element_type=F32)


def dot_nn(a, b):
    return lax.dot_general(a, b, (((1,), (0,)), ((), ())), preferred_element_type=F32)


def pack_kernel(q_ref, k_ref, v_ref, o_ref):
    left = left_lanes((TOK, 2 * HD))
    for pair in range(KVH // 2):
        lanes = slice(pair * 128, pair * 128 + 128)
        keys, values = k_ref[:, lanes], v_ref[:, lanes]
        even = jnp.where(left, keys, swap_halves(values))
        odd = jnp.where(left, swap_halves(keys), values)
        for part in range(PARTS):
            o_ref[2 * pair * PARTS + part, :TOK, :] = even
            o_ref[(2 * pair + 1) * PARTS + part, :TOK, :] = odd
    left = left_lanes((PARTS * HALF, 2 * HD))
    for pair in range(HEADS // 2):
        rows = q_ref[:, pair * 128 : pair * 128 + 128] * jnp.asarray(SCALE, BF16)
        rows = rows.reshape(PARTS, 2, HALF, 128)
        top = rows[:, 0].reshape(PARTS * HALF, 128)
        bottom = rows[:, 1].reshape(PARTS * HALF, 128)
        even = jnp.where(left, top, swap_halves(bottom))
        odd = jnp.where(left, swap_halves(top), bottom)
        for head, packed in ((2 * pair, even), (2 * pair + 1, odd)):
            kv, group = head // GROUP, head % GROUP
            for part in range(PARTS):
                o_ref[
                    kv * PARTS + part, TOK + group * HALF : TOK + (group + 1) * HALF, :
                ] = packed[part * HALF : (part + 1) * HALF]


def pack(query, key, value):
    return pl.pallas_call(
        pack_kernel,
        out_shape=jax.ShapeDtypeStruct((SEQ, PACK, 128), BF16),
        compiler_params=pltpu.CompilerParams(vmem_limit_bytes=32 * MIB),
        name="pack",
    )(query, key, value)


QS = 8
KS = 8
TILE = QS * 2 * QROWS
KBLK = KS * TOK


def attention_kernel(strip_ref, x_ref, o_ref, ones_ref, q_ref, m_ref, acc_ref):
    strip = strip_ref[0]
    for block in range(SEQ // KS):
        kv = x_ref[block * KS : (block + 1) * KS, :TOK, :].reshape(KBLK, 128)
        ones_ref[block] = jnp.where(left_lanes((KBLK, 128)), jnp.asarray(1.0, BF16), kv)
    half = QS * QROWS
    left = left_lanes((half, 128))
    row = lax.broadcasted_iota(jnp.int32, (TILE, KBLK), 0)
    lower = row >= half
    row = jnp.where(lower, row - half, row)
    source = row // QROWS
    inner = row % HALF
    position = source * TOK + strip * STRIP + inner + jnp.where(lower, HALF, 0)
    key_position = lax.broadcasted_iota(jnp.int32, (TILE, KBLK), 1)
    visible = key_position <= position

    def step(block, masked):
        kv = x_ref[pl.ds(block * KS, KS), :TOK, :].reshape(KBLK, 128)
        scores = dot_nt(q_ref[...], kv)
        if masked:
            scores = jnp.where(visible, scores, NEGATIVE)
        before = m_ref[...]
        top = jnp.maximum(before, jnp.max(scores, axis=1, keepdims=True))
        weights = jnp.exp(scores - top[:, :1]).astype(BF16)
        acc_ref[...] = acc_ref[...] * jnp.exp(before - top) + dot_nn(weights, ones_ref[block])
        m_ref[...] = top

    def tile(number, carry):
        packed = x_ref[pl.ds(number * QS, QS), TOK:, :].reshape(half, 128)
        zero = jnp.zeros_like(packed)
        q_ref[:half] = jnp.where(left, packed, zero)
        q_ref[half:] = jnp.where(left, swap_halves(packed), zero)
        m_ref[...] = jnp.full((TILE, 128), NEGATIVE, F32)
        acc_ref[...] = jnp.zeros((TILE, 128), F32)

        def block(index, inner_carry):
            step(index, False)
            return inner_carry

        lax.fori_loop(0, number, block, 0)
        step(number, True)
        total = acc_ref[...]
        result = total / swap_halves(total)
        merged = jnp.where(left, swap_halves(result[:half]), result[half:])
        o_ref[pl.ds(number * QS, QS)] = merged.astype(BF16).reshape(QS, QROWS, 128)
        return carry

    lax.fori_loop(0, SEQ // QS, tile, 0)


def attention(strip, received):
    return pl.pallas_call(
        attention_kernel,
        out_shape=jax.ShapeDtypeStruct((SEQ, QROWS, 128), BF16),
        in_specs=[
            pl.BlockSpec(memory_space=pltpu.SMEM),
            pl.BlockSpec(memory_space=pltpu.VMEM),
        ],
        scratch_shapes=[
            pltpu.VMEM((SEQ // KS, KBLK, 128), BF16),
            pltpu.VMEM((TILE, 128), BF16),
            pltpu.VMEM((TILE, 128), F32),
            pltpu.VMEM((TILE, 128), F32),
        ],
        compiler_params=pltpu.CompilerParams(vmem_limit_bytes=48 * MIB),
        name="attention",
    )(strip, received)


def route_kernel(routes_ref, routes_t_ref, weights_ref, spread_ref, combine_ref):
    routes, routes_t, weights = routes_ref[...], routes_t_ref[...], weights_ref[...]
    expert = lax.broadcasted_iota(jnp.int32, (TOK, EXPERTS), 1)
    expert_t = lax.broadcasted_iota(jnp.int32, (EXPERTS, TOK), 0)
    named = jnp.zeros((TOK, EXPERTS), F32)
    named_t = jnp.zeros((EXPERTS, TOK), F32)
    scale = jnp.zeros((TOK, EXPERTS), F32)
    for k in range(8):
        hit = routes[:, k : k + 1] == expert
        named = jnp.where(hit, 1.0, named)
        scale = jnp.where(hit, weights[:, k : k + 1], scale)
        named_t = jnp.where(routes_t[k : k + 1, :] == expert_t, 1.0, named_t)
    row = lax.broadcasted_iota(jnp.int32, (TOK, TOK), 0)
    col = lax.broadcasted_iota(jnp.int32, (TOK, TOK), 1)
    before = jnp.where(col < row, 1.0, 0.0).astype(BF16)
    before_t = jnp.where(row < col, 1.0, 0.0).astype(BF16)
    slot = jnp.where(named > 0.5, dot_nn(before, named.astype(BF16)), -1.0).astype(BF16)
    slot_t = jnp.where(named_t > 0.5, dot_nn(named_t.astype(BF16), before_t), -1.0).astype(BF16)

    r = lax.broadcasted_iota(jnp.int32, (SLOTS, EXPERTS), 0)
    e = lax.broadcasted_iota(jnp.int32, (SLOTS, EXPERTS), 1) * CAP
    owner = jnp.where((r >= e) & (r < e + CAP), 1.0, 0.0).astype(BF16)
    r = lax.broadcasted_iota(jnp.int32, (SLOTS, TOK), 0).astype(F32)
    place = r - CAP * jnp.floor((r + 0.5) * (1.0 / CAP))
    spread_ref[...] = jnp.where(dot_nn(owner, slot_t) == place, 1.0, 0.0).astype(BF16)

    r = lax.broadcasted_iota(jnp.int32, (EXPERTS, SLOTS), 1)
    e = lax.broadcasted_iota(jnp.int32, (EXPERTS, SLOTS), 0) * CAP
    owner = jnp.where((r >= e) & (r < e + CAP), 1.0, 0.0).astype(BF16)
    r = lax.broadcasted_iota(jnp.int32, (TOK, SLOTS), 1).astype(F32)
    place = r - CAP * jnp.floor((r + 0.5) * (1.0 / CAP))
    chosen = dot_nn(slot, owner) == place
    high = scale.astype(BF16)
    low = (scale - high.astype(F32)).astype(BF16)
    combine_ref[:TOK] = jnp.where(chosen, dot_nn(high, owner), 0.0).astype(BF16)
    combine_ref[TOK:] = jnp.where(chosen, dot_nn(low, owner), 0.0).astype(BF16)


def route(routes, weights):
    return pl.pallas_call(
        route_kernel,
        out_shape=(
            jax.ShapeDtypeStruct((SLOTS, TOK), BF16),
            jax.ShapeDtypeStruct((2 * TOK, SLOTS), BF16),
        ),
        compiler_params=pltpu.CompilerParams(vmem_limit_bytes=32 * MIB),
        name="route",
    )(routes, routes.T, weights)


EXP_STEP = 8
SPREAD_ROWS = EXP_STEP * CAP


def post_kernel(x_ref, w_ref, resid_ref, gain_ref, spread_ref, mid_ref, out_ref, att_ref, norm_ref):
    @pl.when(pl.program_id(0) == 0)
    def _():
        left = left_lanes((PARTS, HALF, 128))
        for pair in range(HEADS // 2):
            pieces = []
            for head in (2 * pair, 2 * pair + 1):
                kv, group = head // GROUP, head % GROUP
                pieces.append(
                    x_ref[kv * PARTS : (kv + 1) * PARTS, group * HALF : (group + 1) * HALF, :]
                )
            even, odd = pieces
            top = jnp.where(left, even, swap_halves(odd))
            bottom = jnp.where(left, swap_halves(even), odd)
            both = jnp.concatenate([top[:, None], bottom[:, None]], axis=1)
            att_ref[:, pair * 128 : pair * 128 + 128] = both.reshape(TOK, 128)
        middle = (resid_ref[...].astype(F32) + dot_nn(att_ref[...], w_ref[...])).astype(BF16)
        mid_ref[...] = middle
        values = middle.astype(F32)
        mean_square = jnp.mean(values * values, axis=-1, keepdims=True)
        norm_ref[...] = (values * lax.rsqrt(mean_square + EPSILON) * gain_ref[...]).astype(BF16)

    out_ref[...] = dot_nn(spread_ref[...], norm_ref[...]).astype(BF16)


def post(received, weight, resid, gain, spread):
    steps = EXPERTS // EXP_STEP
    return pl.pallas_call(
        post_kernel,
        grid=(steps,),
        out_shape=(
            jax.ShapeDtypeStruct((TOK, D), BF16),
            jax.ShapeDtypeStruct((SLOTS, D), BF16),
        ),
        in_specs=[
            pl.BlockSpec((SEQ, QROWS, 128), lambda i: (0, 0, 0)),
            pl.BlockSpec((D, D), lambda i: (0, 0)),
            pl.BlockSpec((TOK, D), lambda i: (0, 0)),
            pl.BlockSpec((1, D), lambda i: (0, 0)),
            pl.BlockSpec((SPREAD_ROWS, TOK), lambda i: (i, 0)),
        ],
        out_specs=(
            pl.BlockSpec((TOK, D), lambda i: (0, 0)),
            pl.BlockSpec((SPREAD_ROWS, D), lambda i: (i, 0)),
        ),
        scratch_shapes=[pltpu.VMEM((TOK, D), BF16), pltpu.VMEM((TOK, D), BF16)],
        compiler_params=pltpu.CompilerParams(vmem_limit_bytes=48 * MIB),
        name="post",
    )(received, weight, resid, gain, spread)


EROWS = 256


def expert_kernel(x_ref, gate_ref, up_ref, down_ref, o_ref):
    rows = x_ref[...]
    gate = dot_nn(rows, gate_ref[...])
    up = dot_nn(rows, up_ref[...])
    hidden = (gate / (1.0 + jnp.exp(-gate)) * up).astype(BF16)
    o_ref[...] = dot_nn(hidden, down_ref[...]).astype(BF16)


def expert(rows, gate, up, down):
    return pl.pallas_call(
        expert_kernel,
        grid=(rows.shape[0] // EROWS,),
        out_shape=jax.ShapeDtypeStruct(rows.shape, BF16),
        in_specs=[
            pl.BlockSpec((EROWS, D), lambda i: (i, 0)),
            pl.BlockSpec((D, FFE), lambda i: (0, 0)),
            pl.BlockSpec((D, FFE), lambda i: (0, 0)),
            pl.BlockSpec((FFE, D), lambda i: (0, 0)),
        ],
        out_specs=pl.BlockSpec((EROWS, D), lambda i: (i, 0)),
        compiler_params=pltpu.CompilerParams(vmem_limit_bytes=48 * MIB),
        name="expert",
    )(rows, gate, up, down)


CCOLS = 512


def combine_kernel(c_ref, x_ref, mid_ref, o_ref):
    both = dot_nn(c_ref[...], x_ref[...])
    o_ref[...] = (mid_ref[...].astype(F32) + (both[:TOK] + both[TOK:])).astype(BF16)


def combine(matrix, rows, middle):
    return pl.pallas_call(
        combine_kernel,
        grid=(D // CCOLS,),
        out_shape=jax.ShapeDtypeStruct((TOK, D), BF16),
        in_specs=[
            pl.BlockSpec((2 * TOK, SLOTS), lambda i: (0, 0)),
            pl.BlockSpec((SLOTS, CCOLS), lambda i: (0, i)),
            pl.BlockSpec((TOK, CCOLS), lambda i: (0, i)),
        ],
        out_specs=pl.BlockSpec((TOK, CCOLS), lambda i: (0, i)),
        compiler_params=pltpu.CompilerParams(vmem_limit_bytes=48 * MIB),
        name="combine",
    )(matrix, rows, middle)


DROWS = KVH * 8


def decode_kernel(info_ref, q_ref, kn_ref, vn_ref, k_ref, v_ref, o_ref):
    request = pl.program_id(0)
    seq = info_ref[0]
    length = info_ref[1 + request]
    query = q_ref[0]
    position = seq * CBLK + lax.broadcasted_iota(jnp.int32, (DROWS, CBLK), 1)
    visible = position < length
    scores = jnp.where(visible, dot_nt(query, k_ref[0]) * SCALE, NEGATIVE)
    first = jnp.where(seq == 0, 1.0, 0.0)
    product = query.astype(F32) * kn_ref[0].astype(F32)
    fresh = jnp.sum(product, axis=1, keepdims=True) * SCALE
    fresh = jnp.where(first > 0.5, fresh, NEGATIVE)
    top = jnp.maximum(jnp.max(scores, axis=1, keepdims=True), fresh)
    weights = jnp.where(visible, jnp.exp(scores - top), 0.0)
    fresh_weight = jnp.exp(fresh - top) * first
    total = jnp.sum(weights, axis=1, keepdims=True) + fresh_weight
    fresh_round = fresh_weight.astype(BF16).astype(F32)
    weighted = dot_nn(weights.astype(BF16), v_ref[0]) + fresh_round * vn_ref[0].astype(F32)
    lane = lax.broadcasted_iota(jnp.int32, (8, 128), 1)
    for kv in range(KVH):
        rows = slice(8 * kv, 8 * kv + 8)
        lanes = slice(128 * (kv // 2), 128 * (kv // 2) + 128)
        piece = weighted[rows, lanes]
        if kv % 2:
            piece = swap_halves(piece)
        piece = jnp.where(lane < HD, piece, jnp.where(lane < 96, top[rows], total[rows]))
        o_ref[kv] = piece


def decode(info, query, key_new, value_new, key_cache, value_cache):
    return pl.pallas_call(
        decode_kernel,
        grid=(RLOC,),
        out_shape=jax.ShapeDtypeStruct((SEQ, 8, 128), F32),
        in_specs=[
            pl.BlockSpec(memory_space=pltpu.SMEM),
            pl.BlockSpec((1, DROWS, KVH * HD), lambda i: (i, 0, 0)),
            pl.BlockSpec((1, 1, KVH * HD), lambda i: (i, 0, 0)),
            pl.BlockSpec((1, 1, KVH * HD), lambda i: (i, 0, 0)),
            pl.BlockSpec((1, CBLK, KVH * HD), lambda i: (i, 0, 0)),
            pl.BlockSpec((1, CBLK, KVH * HD), lambda i: (i, 0, 0)),
        ],
        out_specs=pl.BlockSpec((KVH, 8, 128), lambda i: (i, 0, 0)),
        compiler_params=pltpu.CompilerParams(vmem_limit_bytes=48 * MIB),
        name="decode",
    )(info, query, key_new, value_new, key_cache, value_cache)


def exchange(x):
    return lax.all_to_all(x, "seq", split_axis=0, concat_axis=0, tiled=True)


def gather_req(shard, axis):
    index = lax.axis_index("req")
    across = lax.ppermute(shard, "req", [(i, i ^ 2) for i in range(4)])
    own_pair = lax.ppermute(shard, "req", [(i, i ^ 1) for i in range(4)])
    far_pair = lax.ppermute(across, "req", [(i, i ^ 1) for i in range(4)])
    size = shard.shape[axis]
    shape = list(shard.shape)
    shape[axis] = 4 * size
    full = jnp.zeros(shape, shard.dtype)
    for piece, flip in ((shard, 0), (own_pair, 1), (across, 2), (far_pair, 3)):
        full = lax.dynamic_update_slice_in_dim(full, piece, (index ^ flip) * size, axis)
    return full


def block_query(dec_query):
    rows = dec_query.reshape(RLOC, KVH, GROUP, HD)
    rows = jnp.pad(rows, ((0, 0), (0, 0), (0, 8 - GROUP), (0, 0)))
    same = jnp.eye(KVH, dtype=BF16)[None, :, None, :, None]
    return (rows[:, :, :, None, :] * same).reshape(RLOC, DROWS, KVH * HD)


def body(
    prefill_query,
    prefill_key,
    prefill_value,
    prefill_resid,
    dec_query,
    dec_key_new,
    dec_value_new,
    dec_resid,
    cache_lengths,
    key_cache,
    value_cache,
    attn_out_weight,
    ffn_gain,
    expert_gate,
    expert_up,
    expert_down,
    routes,
    route_weights,
):
    seq = lax.axis_index("seq").astype(jnp.int32)
    strip = (seq % PARTS).reshape(1)
    received = exchange(pack(prefill_query, prefill_key, prefill_value))
    gate_up = jnp.concatenate([expert_gate[0], expert_up[0]], axis=1)
    gate_up = gather_req(gate_up, 0)
    gate, up = gate_up[:, :FFE], gate_up[:, FFE:]
    down = gather_req(expert_down[0], 1)
    spread, matrix = route(routes, route_weights)
    info = jnp.concatenate([seq.reshape(1), cache_lengths])
    partial = decode(
        info,
        block_query(dec_query),
        dec_key_new.reshape(RLOC, 1, KVH * HD),
        dec_value_new.reshape(RLOC, 1, KVH * HD),
        key_cache,
        value_cache,
    )
    attended = exchange(attention(strip, received))
    middle, outgoing = post(attended, attn_out_weight, prefill_resid, ffn_gain[None, :], spread)
    incoming = exchange(outgoing.reshape(EXPERTS, CAP, D)).reshape(SLOTS, D)
    result = expert(incoming, gate, up, down)
    returned = exchange(result.reshape(EXPERTS, CAP, D)).reshape(SLOTS, D)
    prefill_out = combine(matrix, returned, middle)

    parts = exchange(partial)
    tops = parts[..., HD : HD + 1]
    top = jnp.max(tops, axis=0, keepdims=True)
    merged = jnp.sum(parts * jnp.exp(tops - top), axis=0)
    decoded = (merged[:, :HD] / merged[:, 96:97]).astype(BF16)
    decoded = jnp.pad(decoded, ((0, 0), (0, 128 - HD)))
    decoded = exchange(jnp.broadcast_to(decoded[None], (SEQ, 8, 128)))
    decoded = decoded[:, :GROUP, :HD].reshape(RLOC, HEADS * HD)
    dec_out = (
        dec_resid.astype(F32) + jnp.dot(decoded, attn_out_weight, preferred_element_type=F32)
    ).astype(BF16)
    return (prefill_out, dec_out)


def solution(mesh):
    return jax.shard_map(
        body,
        mesh=mesh,
        in_specs=(
            P(("req", "seq"), None),
            P(("req", "seq"), None),
            P(("req", "seq"), None),
            P(("req", "seq"), None),
            P("req", None),
            P("req", None),
            P("req", None),
            P("req", None),
            P("req"),
            P("req", "seq", None),
            P("req", "seq", None),
            P(),
            P(),
            P("seq", "req", None),
            P("seq", "req", None),
            P("seq", None, "req"),
            P(("req", "seq"), None),
            P(("req", "seq"), None),
        ),
        out_specs=(P(("req", "seq"), None), P("req", None)),
        check_vma=False,
    )
```

time: 823 us -> 269 us (0.33)
  blocking collectives: 382 us -> 0 us
  matrix products: 88 us -> 3.66 us
  waiting for transfers between devices: 204 us -> 138 us
  other arithmetic: 52 us -> 2.41 us
  Pallas kernels: 0 us -> 48.2 us
  local copies, waits for them, and re-layouts: 67.1 us -> 22.7 us
  starting transfers between devices: 13 us -> 52.1 us
  between operations: 14.1 us -> 0.96 us
    pmax x1 -> x0, blocking collectives: 206 us -> none  [decode_attention(): maxima = lax.pmax(local_maxima, 'seq')]
    psum x1 -> x0, blocking collectives: 176 us -> none  [decode_attention(): totals, weighted = lax.psum((totals, weighted), 'seq')]
    all_gather x5 -> x0, waiting for transfers between devices: 149 us -> none  [the longest x1 75.9 us: prefill_attention(): value_rows = lax.all_gather(prefill_value, 'seq', axis=0, tiled=True)]
    dot_general x23 -> x1, matrix products: 88 us -> 3.66 us  [body(): jnp.dot(decoded, attn_out_weight, preferred_element_type=F32)]
    ppermute x0 -> x6, waiting for transfers between devices: none -> 58.1 us  [the longest x2 58.1 us: gather_req(): across = lax.ppermute(shard, 'req', [(i, i ^ 2) for i in range(4)])]
    pallas_call x0 -> x7, Pallas kernels: none -> 48.2 us  [the longest x1 21 us: attention(): pl.pallas_call(attention_kernel, out_shape=jax.ShapeDtypeStruct((SEQ, QRO...]
    reduce_sum x11 -> x1, other arithmetic: 38.5 us -> 0.12 us  [body(): merged = jnp.sum(parts * jnp.exp(tops - top), axis=0)]
    all_to_all x2 -> x6, starting transfers between devices: 12.6 us -> 49.3 us  [exchange(): return lax.all_to_all(x, 'seq', split_axis=0, concat_axis=0, tiled=True)]
  transfers between devices with their start and end apart: 7 -> 12, of which waited for: 3 -> 5; matrix products, arithmetic and copies ran while one was open for 21% -> 8% of each run, Pallas kernels for 0% -> 8%
where the time goes in v1:
time: 269 us; the launch traced here: 268 us
  waiting for transfers between devices  138 us (51%)
  starting transfers between devices  52.1 us (19%)
  Pallas kernels  48.2 us (18%)
  local copies, waits for them, and re-layouts  22.7 us (8%)
  matrix products  3.66 us (1%)
    all_to_all x6, waiting for transfers between devices, exchange(): return lax.all_to_all(x, 'seq', split_axis=0, concat_axis=0, tiled=True)  79.4 us
    ppermute x2, waiting for transfers between devices, gather_req(): across = lax.ppermute(shard, 'req', [(i, i ^ 2) for i in range(4)])  58.1 us
    all_to_all x6, starting transfers between devices, exchange(): return lax.all_to_all(x, 'seq', split_axis=0, concat_axis=0, tiled=True)  49.3 us
    pallas_call x1, Pallas kernels, attention(): pl.pallas_call(attention_kernel, out_shape=jax.ShapeDtypeStruct((SEQ, QRO...  21 us
    pallas_call x1, Pallas kernels, expert(): pl.pallas_call(expert_kernel, grid=(rows.shape[0] // EROWS,), out_shape=j...  9.5 us
    dynamic_update_slice x7, local copies, waits for them, and re-layouts, gather_req(): lax.dynamic_update_slice_in_dim(full, piece, (index ^ flip) * size, axis)  8.37 us
    unnamed x34, local copies, waits for them, and re-layouts  7.1 us
    pallas_call x1, Pallas kernels, decode(): pl.pallas_call(decode_kernel, grid=(RLOC,), out_shape=jax.ShapeDtypeStruc...  5.84 us
  transfers between devices with their start and end apart: 12, of which 5 were waited for; matrix products, arithmetic and copies ran while one was open for 8% of the time, Pallas kernels for 8%

profile of v1, /device:TPU:0, one launch (start us, length us, event | category | flops | bytes accessed | tf_op | source)
XLA Modules:
  0.0 267.6 jit_solution(1920429967704526472)
XLA Ops:
  0.6 1.0 copy-done.2
  1.6 0.9 copy-done.4
  2.5 0.9 copy-done.5
  3.4 1.4 pack.1
  4.9 10.9 %all-to-all-start = ((bf16[32,176,128]{2,1,0:T(8,128)(2,1)}), bf16[32,176,128]{2,1,0:T(8,128)(2,1)S(1)}, u32[]{:S(2)}, u32[]{:S(2)}) async-start(bf16[32,176,128]{2,1,0:T(8,128)(2,1)} %pack.1), calls=%async_computation | async-start | bytes 2883584 | tf_op jit(solution)/shard_map/all_to_all | solution.py:370
  15.8 23.5 %all-to-all-done.x_ref = bf16[32,176,128]{2,1,0:T(8,128)(2,1)S(1)} async-done(((bf16[32,176,128]{2,1,0:T(8,128)(2,1)}), bf16[32,176,128]{2,1,0:T(8,128)(2,1)S(1)}, u32[]{:S(2)}, u32[]{:S(2)}) %all-to-all-start) | async-done | bytes 1441824 | tf_op jit(solution)/shard_map/all_to_all | solution.py:370
  39.3 21.0 %attention.1 = bf16[32,48,128]{2,1,0:T(8,128)(2,1)} custom-call(s32[1]{0:T(128)} %bitcast.1.strip_ref, bf16[32,176,128]{2,1,0:T(8,128)(2,1)S(1)} %all-to-all-done.x_ref), custom_call_target="tpu_custom_call" | custom-call | tf_op jit(solution)/shard_map/attention/pallas_call | solution.py:143
  60.4 4.2 %all-to-all-start.1 = ((bf16[32,48,128]{2,1,0:T(8,128)(2,1)}), bf16[32,48,128]{2,1,0:T(8,128)(2,1)S(1)}, u32[]{:S(2)}, u32[]{:S(2)}) async-start(bf16[32,48,128]{2,1,0:T(8,128)(2,1)} %attention.1), calls=%async_computation.1 | async-start | bytes 786432 | tf_op jit(solution)/shard_map/all_to_all | solution.py:370
  64.7 0.1 mul.50
  64.8 0.3 mul.51
  65.3 0.1 mul.53
  65.6 2.2 copy-done
  67.8 5.8 %decode.1 = f32[32,8,128]{2,1,0:T(8,128)} custom-call(s32[5]{0:T(128)S(1)} %pad_add_fusion.info_ref, bf16[4,64,512]{2,1,0:T(8,128)(2,1)S(1)} %broadcast_multiply_fusion.q_ref, bf16[4,1,512]{2,1,0:T(2,128)(2,1)S(1)} %copy.44.kn_ref, bf16[4,1,512]{2,1,0:T(2,128)(2,1)S(1)} %copy.45.vn_ref, bf16[4,1024,512]{2,1,0:T(8,128)(2,1)S(1)} %copy-done, ...), custom_call_target="tpu_custom_call" | custom-call | tf_op jit(solution)/shard_map/decode/pallas_call | solution.py:351
  73.6 2.6 all-to-all-done.1.x_ref
  76.2 7.2 %all-to-all-start.4 = ((f32[32,8,128]{2,1,0:T(8,128)}), f32[32,8,128]{2,1,0:T(8,128)S(1)}, u32[]{:S(2)}, u32[]{:S(2)}) async-start(f32[32,8,128]{2,1,0:T(8,128)} %decode.1), calls=%async_computation.4 | async-start | bytes 262144 | tf_op jit(solution)/shard_map/all_to_all | solution.py:370
  83.4 0.1 copy.42.routes_ref
  83.7 1.0 route.1
  84.6 5.0 %post.1 = (bf16[128,1536]{1,0:T(8,128)(2,1)S(1)}, bf16[1280,1536]{1,0:T(8,128)(2,1)S(1)}) custom-call(bf16[32,48,128]{2,1,0:T(8,128)(2,1)S(1)} %all-to-all-done.1.x_ref, bf16[1536,1536]{1,0:T(8,128)(2,1)} %w_ref.1, bf16[128,1536]{1,0:T(8,128)(2,1)S(1)} %copy-done.3, f32[1,1536]{1,0:T(1,128)S(1)} %broadcast_in_dim.8.gain_ref, ...), custom_call_target="tpu_custom_call" | custom-call | tf_op jit(solution)/shard_map/post/pallas_call | solution.py:242
  89.7 1.9 copy-done.1
  91.5 2.1 all-to-all-done.4
  93.6 7.8 %all-to-all-start.2 = ((bf16[32,40,1536]{2,1,0:T(8,128)(2,1)}), bf16[32,40,1536]{2,1,0:T(8,128)(2,1)}, u32[]{:S(2)}, u32[]{:S(2)}) async-start(bf16[32,40,1536]{2,1,0:T(8,128)(2,1)} %bitcast.21), calls=%async_computation.2 | async-start | bytes 7864320 | tf_op jit(solution)/shard_map/all_to_all | solution.py:370
  101.5 2.2 broadcast_in_dim.9
  103.7 1.1 pad_maximum_fusion
  104.8 1.0 collective-permute-start.1
  105.8 0.2 collective-permute-start.3
  106.0 1.1 collective-permute-start.4
  107.0 0.1 broadcast_in_dim.20
  107.1 1.1 constant_dynamic-update-slice_fusion.3
  108.2 0.2 slice_reduce_fusion
  108.4 0.8 subtract_exponential_fusion
  109.2 1.1 copy.49
  110.3 0.1 multiply_reduce_fusion
  110.5 0.2 slice_reduce_fusion.1
  110.7 58.1 %collective-permute-done.4 = bf16[512,384]{1,0:T(8,128)(2,1)} collective-permute-done((bf16[512,384]{1,0:T(8,128)(2,1)}, bf16[512,384]{1,0:T(8,128)(2,1)}, u32[]{:S(2)}, u32[]{:S(2)}) %collective-permute-start.4) | collective-permute-done | bytes 393248 | tf_op jit(solution)/shard_map/ppermute | solution.py:375
  168.8 0.5 collective-permute-start.2
  169.4 1.1 constant_dynamic-update-slice_fusion.2
  170.5 1.1 constant_dynamic-update-slice_fusion.1
  171.6 2.1 constant_dynamic-update-slice_fusion.6
  173.7 2.1 constant_dynamic-update-slice_fusion.5
  175.8 1.0 constant_dynamic-update-slice_fusion.4
  176.7 0.6 broadcast_in_dim.21
  177.4 9.2 %all-to-all-start.5 = ((bf16[32,8,128]{2,1,0:T(8,128)(2,1)}), bf16[32,8,128]{2,1,0:T(8,128)(2,1)S(1)}, u32[]{:S(2)}, u32[]{:S(2)}) async-start(bf16[32,8,128]{2,1,0:T(8,128)(2,1)} %broadcast_in_dim.21), calls=%async_computation.5 | async-start | bytes 131072 | tf_op jit(solution)/shard_map/all_to_all | solution.py:370
  186.6 2.1 fusion.2
  188.7 9.5 %expert.1 = bf16[1280,1536]{1,0:T(8,128)(2,1)} custom-call(bf16[1280,1536]{1,0:T(8,128)(2,1)} %bitcast.3.x_ref, bf16[1536,512]{1,0:T(8,128)(2,1)S(1)} %get-tuple-element.11.gate_ref, bf16[1536,512]{1,0:T(8,128)(2,1)S(1)} %get-tuple-element.10.up_ref, bf16[512,1536]{1,0:T(8,128)(2,1)S(1)} %constant_dynamic-update-slice_fusion.down_ref), custom_call_target="tpu_custom_call" | custom-call | tf_op jit(solution)/shard_map/expert/pallas_call | solution.py:278
  198.2 10.0 %all-to-all-start.3 = ((bf16[32,40,1536]{2,1,0:T(8,128)(2,1)}), bf16[32,40,1536]{2,1,0:T(8,128)(2,1)}, u32[]{:S(2)}, u32[]{:S(2)}) async-start(bf16[32,40,1536]{2,1,0:T(8,128)(2,1)} %bitcast.23), calls=%async_computation.3 | async-start | bytes 7864320 | tf_op jit(solution)/shard_map/all_to_all | solution.py:370
  208.4 3.7 %fusion = bf16[4,1536]{1,0:T(4,128)(2,1)} fusion(bf16[4,1536]{1,0:T(4,128)(2,1)S(1)} %reshape.61, bf16[1536,1536]{1,0:T(8,128)(2,1)} %w_ref.1, bf16[4,1536]{1,0:T(4,128)(2,1)S(1)} %copy-done.10), kind=kOutput, calls=%fused_computation.1 | convolution fusion | flops 18892800 | bytes 4755456 | tf_op jit(solution)/shard_map/dot_general | solution.py:447
  212.0 51.2 %all-to-all-done.3 = bf16[32,40,1536]{2,1,0:T(8,128)(2,1)} async-done(((bf16[32,40,1536]{2,1,0:T(8,128)(2,1)}), bf16[32,40,1536]{2,1,0:T(8,128)(2,1)}, u32[]{:S(2)}, u32[]{:S(2)}) %all-to-all-start.3) | async-done | bytes 3932192 | tf_op jit(solution)/shard_map/all_to_all | solution.py:370
  263.2 4.4 %combine.1 = bf16[128,1536]{1,0:T(8,128)(2,1)} custom-call(bf16[256,1280]{1,0:T(8,128)(2,1)S(1)} %get-tuple-element.6.c_ref, bf16[1280,1536]{1,0:T(8,128)(2,1)} %bitcast.8.x_ref, bf16[128,1536]{1,0:T(8,128)(2,1)S(1)} %get-tuple-element.9.mid_ref), custom_call_target="tpu_custom_call" | custom-call | tf_op jit(solution)/shard_map/combine/pallas_call | solution.py:303
  (51 shorter events, 0.8 us)
Async XLA Ops:
  0.6 1.0 copy-start.2
  1.6 0.9 copy-start.4
  2.5 0.9 copy-start.5
  4.9 59.7 %copy-start.9 = (bf16[4,1536]{1,0:T(4,128)(2,1)S(1)}, bf16[4,1536]{1,0:T(4,128)(2,1)}, u32[]{:S(2)}) copy-start(bf16[4,1536]{1,0:T(4,128)(2,1)} %param.22) | copy-start | bytes 36868
  4.9 60.5 %copy-start.12 = (bf16[4,512]{1,0:T(4,128)(2,1)S(1)}, bf16[4,512]{1,0:T(4,128)(2,1)}, u32[]{:S(2)}) copy-start(bf16[4,512]{1,0:T(4,128)(2,1)} %param.23) | copy-start | bytes 12292
  4.9 60.5 %copy-start.13 = (bf16[4,512]{1,0:T(4,128)(2,1)S(1)}, bf16[4,512]{1,0:T(4,128)(2,1)}, u32[]{:S(2)}) copy-start(bf16[4,512]{1,0:T(4,128)(2,1)} %param.24) | copy-start | bytes 12292
  4.9 60.6 %copy-start.15 = (s32[4]{0:T(128)S(1)}, s32[4]{0:T(128)}, u32[]{:S(2)}) copy-start(s32[4]{0:T(128)} %param.26) | copy-start | bytes 52
  4.9 34.4 %all-to-all-start = ((bf16[32,176,128]{2,1,0:T(8,128)(2,1)}), bf16[32,176,128]{2,1,0:T(8,128)(2,1)S(1)}, u32[]{:S(2)}, u32[]{:S(2)}) async-start(bf16[32,176,128]{2,1,0:T(8,128)(2,1)} %pack.1), calls=%async_computation | async-start | bytes 2883584 | tf_op jit(solution)/shard_map/all_to_all | solution.py:370
  60.4 15.8 %all-to-all-start.1 = ((bf16[32,48,128]{2,1,0:T(8,128)(2,1)}), bf16[32,48,128]{2,1,0:T(8,128)(2,1)S(1)}, u32[]{:S(2)}, u32[]{:S(2)}) async-start(bf16[32,48,128]{2,1,0:T(8,128)(2,1)} %attention.1), calls=%async_computation.1 | async-start | bytes 786432 | tf_op jit(solution)/shard_map/all_to_all | solution.py:370
  65.6 2.2 copy-start
  67.8 15.7 %copy-start.6 = (s32[128,8]{0,1:T(8,128)S(1)}, s32[128,8]{0,1:T(8,128)}, u32[]{:S(2)}) copy-start(s32[128,8]{0,1:T(8,128)} %param.34) | copy-start | bytes 12292
  67.8 15.8 %copy-start.14 = (f32[128,8]{0,1:T(8,128)S(1)}, f32[128,8]{0,1:T(8,128)}, u32[]{:S(2)}) copy-start(f32[128,8]{0,1:T(8,128)} %param.35) | copy-start | bytes 12292
  67.8 15.9 %copy-start.11 = (f32[1536]{0:T(1024)S(1)}, f32[1536]{0:T(1024)}, u32[]{:S(2)}) copy-start(f32[1536]{0:T(1024)} %param.30) | copy-start | bytes 18436
  67.8 16.9 %copy-start.3 = (bf16[128,1536]{1,0:T(8,128)(2,1)S(1)}, bf16[128,1536]{1,0:T(8,128)(2,1)}, u32[]{:S(2)}) copy-start(bf16[128,1536]{1,0:T(8,128)(2,1)} %resid_ref.1) | copy-start | bytes 1179652
  76.2 17.4 %all-to-all-start.4 = ((f32[32,8,128]{2,1,0:T(8,128)}), f32[32,8,128]{2,1,0:T(8,128)S(1)}, u32[]{:S(2)}, u32[]{:S(2)}) async-start(f32[32,8,128]{2,1,0:T(8,128)} %decode.1), calls=%async_computation.4 | async-start | bytes 262144 | tf_op jit(solution)/shard_map/all_to_all | solution.py:370
  89.7 1.9 copy-start.1
  93.6 83.1 %all-to-all-start.2 = ((bf16[32,40,1536]{2,1,0:T(8,128)(2,1)}), bf16[32,40,1536]{2,1,0:T(8,128)(2,1)}, u32[]{:S(2)}, u32[]{:S(2)}) async-start(bf16[32,40,1536]{2,1,0:T(8,128)(2,1)} %bitcast.21), calls=%async_computation.2 | async-start | bytes 7864320 | tf_op jit(solution)/shard_map/all_to_all | solution.py:370
  101.5 2.2 copy-start.7
  101.5 2.2 copy-start.8
  104.8 66.8 %collective-permute-start = (bf16[384,1024]{1,0:T(8,128)(2,1)S(1)}, bf16[384,1024]{1,0:T(8,128)(2,1)}, u32[]{:S(2)}, u32[]{:S(2)}) collective-permute-start(bf16[384,1024]{1,0:T(8,128)(2,1)S(1)} %get-tuple-element.12), channel_id=1, source_target_pairs={{0,32},{32,0},{64,96},{96,64},{1,33},{33,1},{65,97},{97,65},{2,34}... | collective-permute-start | bytes 2359304 | tf_op jit(solution)/shard_map/ppermute | solution.py:376
  104.8 64.0 %collective-permute-start.1 = (bf16[384,1024]{1,0:T(8,128)(2,1)S(1)}, bf16[384,1024]{1,0:T(8,128)(2,1)}, u32[]{:S(2)}, u32[]{:S(2)}) collective-permute-start(bf16[384,1024]{1,0:T(8,128)(2,1)S(1)} %get-tuple-element.12), channel_id=1, source_target_pairs={{0,64},{32,96},{64,0},{96,32},{1,65},{33,97},{65,1},{97,33},{2,66}... | collective-permute-start | bytes 2359304 | tf_op jit(solution)/shard_map/ppermute | solution.py:375
  105.8 63.6 %collective-permute-start.3 = (bf16[512,384]{1,0:T(8,128)(2,1)}, bf16[512,384]{1,0:T(8,128)(2,1)}, u32[]{:S(2)}, u32[]{:S(2)}) collective-permute-start(bf16[512,384]{1,0:T(8,128)(2,1)} %bitcast.6), channel_id=1, source_target_pairs={{0,32},{32,0},{64,96},{96,64},{1,33},{33,1},{65,97},{97,65},{2,34}... | collective-permute-start | bytes 1179656 | tf_op jit(solution)/shard_map/ppermute | solution.py:376
  106.0 62.8 %collective-permute-start.4 = (bf16[512,384]{1,0:T(8,128)(2,1)}, bf16[512,384]{1,0:T(8,128)(2,1)}, u32[]{:S(2)}, u32[]{:S(2)}) collective-permute-start(bf16[512,384]{1,0:T(8,128)(2,1)} %bitcast.6), channel_id=1, source_target_pairs={{0,64},{32,96},{64,0},{96,32},{1,65},{33,97},{65,1},{97,33},{2,66}... | collective-permute-start | bytes 1179656 | tf_op jit(solution)/shard_map/ppermute | solution.py:375
  168.8 2.7 %collective-permute-start.5 = (bf16[512,384]{1,0:T(8,128)(2,1)}, bf16[512,384]{1,0:T(8,128)(2,1)S(1)}, u32[]{:S(2)}, u32[]{:S(2)}) collective-permute-start(bf16[512,384]{1,0:T(8,128)(2,1)} %collective-permute-done.4), channel_id=1, source_target_pairs={{0,32},{32,0},{64,96},{96,64},{1,33},{33,1},{65,97},{97,65},{2,34}... | collective-permute-start | bytes 1179656 | tf_op jit(solution)/shard_map/ppermute | solution.py:377
  168.8 7.0 %collective-permute-start.2 = (bf16[384,1024]{1,0:T(8,128)(2,1)}, bf16[384,1024]{1,0:T(8,128)(2,1)S(1)}, u32[]{:S(2)}, u32[]{:S(2)}) collective-permute-start(bf16[384,1024]{1,0:T(8,128)(2,1)} %collective-permute-done.1), channel_id=1, source_target_pairs={{0,32},{32,0},{64,96},{96,64},{1,33},{33,1},{65,97},{97,65},{2,34}... | collective-permute-start | bytes 2359304 | tf_op jit(solution)/shard_map/ppermute | solution.py:377
  177.4 20.8 %all-to-all-start.5 = ((bf16[32,8,128]{2,1,0:T(8,128)(2,1)}), bf16[32,8,128]{2,1,0:T(8,128)(2,1)S(1)}, u32[]{:S(2)}, u32[]{:S(2)}) async-start(bf16[32,8,128]{2,1,0:T(8,128)(2,1)} %broadcast_in_dim.21), calls=%async_computation.5 | async-start | bytes 131072 | tf_op jit(solution)/shard_map/all_to_all | solution.py:370
  198.2 10.2 %copy-start.10 = (bf16[4,1536]{1,0:T(4,128)(2,1)S(1)}, bf16[4,1536]{1,0:T(4,128)(2,1)}, u32[]{:S(2)}) copy-start(bf16[4,1536]{1,0:T(4,128)(2,1)} %param.25) | copy-start | bytes 36868
  198.2 65.0 %all-to-all-start.3 = ((bf16[32,40,1536]{2,1,0:T(8,128)(2,1)}), bf16[32,40,1536]{2,1,0:T(8,128)(2,1)}, u32[]{:S(2)}, u32[]{:S(2)}) async-start(bf16[32,40,1536]{2,1,0:T(8,128)(2,1)} %bitcast.23), calls=%async_computation.3 | async-start | bytes 7864320 | tf_op jit(solution)/shard_map/all_to_all | solution.py:370

commit v2 on v1

--- a/solution.py
+++ b/solution.py
@@ -20,6 +20,7 @@
 HALF = STRIP // 2
 QROWS = GROUP * HALF
 PACK = TOK + QROWS
+BACK = QROWS + 8
 SLOTS = EXPERTS * CAP
 CBLK = 1024
 RLOC = 4
@@ -48,18 +49,20 @@
     return lax.dot_general(a, b, (((1,), (0,)), ((), ())), preferred_element_type=F32)
 
 
+PACK_STEPS = 4
+PAIRS = HEADS // 2 // PACK_STEPS
+
+
 def pack_kernel(q_ref, k_ref, v_ref, o_ref):
     left = left_lanes((TOK, 2 * HD))
-    for pair in range(KVH // 2):
-        lanes = slice(pair * 128, pair * 128 + 128)
-        keys, values = k_ref[:, lanes], v_ref[:, lanes]
-        even = jnp.where(left, keys, swap_halves(values))
-        odd = jnp.where(left, swap_halves(keys), values)
-        for part in range(PARTS):
-            o_ref[2 * pair * PARTS + part, :TOK, :] = even
-            o_ref[(2 * pair + 1) * PARTS + part, :TOK, :] = odd
+    keys, values = k_ref[...], v_ref[...]
+    even = jnp.where(left, keys, swap_halves(values))
+    odd = jnp.where(left, swap_halves(keys), values)
+    for part in range(PARTS):
+        o_ref[part, :TOK, :] = even
+        o_ref[PARTS + part, :TOK, :] = odd
     left = left_lanes((PARTS * HALF, 2 * HD))
-    for pair in range(HEADS // 2):
+    for pair in range(PAIRS):
         rows = q_ref[:, pair * 128 : pair * 128 + 128] * jnp.asarray(SCALE, BF16)
         rows = rows.reshape(PARTS, 2, HALF, 128)
         top = rows[:, 0].reshape(PARTS * HALF, 128)
@@ -77,7 +80,14 @@
 def pack(query, key, value):
     return pl.pallas_call(
         pack_kernel,
+        grid=(PACK_STEPS,),
         out_shape=jax.ShapeDtypeStruct((SEQ, PACK, 128), BF16),
+        in_specs=[
+            pl.BlockSpec((TOK, PAIRS * 128), lambda i: (0, i)),
+            pl.BlockSpec((TOK, 128), lambda i: (0, i)),
+            pl.BlockSpec((TOK, 128), lambda i: (0, i)),
+        ],
+        out_specs=pl.BlockSpec((SEQ // PACK_STEPS, PACK, 128), lambda i: (i, 0, 0)),
         compiler_params=pltpu.CompilerParams(vmem_limit_bytes=32 * MIB),
         name="pack",
     )(query, key, value)
@@ -89,8 +99,9 @@
 KBLK = KS * TOK
 
 
-def attention_kernel(strip_ref, x_ref, o_ref, ones_ref, q_ref, m_ref, acc_ref):
+def attention_kernel(strip_ref, x_ref, dec_ref, o_ref, ones_ref, q_ref, m_ref, acc_ref):
     strip = strip_ref[0]
+    o_ref[:, QROWS:, :] = dec_ref[...]
     for block in range(SEQ // KS):
         kv = x_ref[block * KS : (block + 1) * KS, :TOK, :].reshape(KBLK, 128)
         ones_ref[block] = jnp.where(left_lanes((KBLK, 128)), jnp.asarray(1.0, BF16), kv)
@@ -133,18 +144,19 @@
         total = acc_ref[...]
         result = total / swap_halves(total)
         merged = jnp.where(left, swap_halves(result[:half]), result[half:])
-        o_ref[pl.ds(number * QS, QS)] = merged.astype(BF16).reshape(QS, QROWS, 128)
+        o_ref[pl.ds(number * QS, QS), :QROWS, :] = merged.astype(BF16).reshape(QS, QROWS, 128)
         return carry
 
     lax.fori_loop(0, SEQ // QS, tile, 0)
 
 
-def attention(strip, received):
+def attention(strip, received, partial):
     return pl.pallas_call(
         attention_kernel,
-        out_shape=jax.ShapeDtypeStruct((SEQ, QROWS, 128), BF16),
+        out_shape=jax.ShapeDtypeStruct((SEQ, BACK, 128), BF16),
         in_specs=[
             pl.BlockSpec(memory_space=pltpu.SMEM),
+            pl.BlockSpec(memory_space=pltpu.VMEM),
             pl.BlockSpec(memory_space=pltpu.VMEM),
         ],
         scratch_shapes=[
@@ -155,7 +167,7 @@
         ],
         compiler_params=pltpu.CompilerParams(vmem_limit_bytes=48 * MIB),
         name="attention",
-    )(strip, received)
+    )(strip, received, partial)
 
 
 def route_kernel(routes_ref, routes_t_ref, weights_ref, spread_ref, combine_ref):
@@ -247,7 +259,7 @@
             jax.ShapeDtypeStruct((SLOTS, D), BF16),
         ),
         in_specs=[
-            pl.BlockSpec((SEQ, QROWS, 128), lambda i: (0, 0, 0)),
+            pl.BlockSpec((SEQ, BACK, 128), lambda i: (0, 0, 0)),
             pl.BlockSpec((D, D), lambda i: (0, 0)),
             pl.BlockSpec((TOK, D), lambda i: (0, 0)),
             pl.BlockSpec((1, D), lambda i: (0, 0)),
@@ -266,29 +278,26 @@
 EROWS = 256
 
 
-def expert_kernel(x_ref, gate_ref, up_ref, down_ref, o_ref):
-    rows = x_ref[...]
-    gate = dot_nn(rows, gate_ref[...])
-    up = dot_nn(rows, up_ref[...])
+def expert_kernel(x_ref, w_ref, o_ref):
+    both = dot_nn(x_ref[...], w_ref[:, : 2 * FFE])
+    gate, up = both[:, :FFE], both[:, FFE:]
     hidden = (gate / (1.0 + jnp.exp(-gate)) * up).astype(BF16)
-    o_ref[...] = dot_nn(hidden, down_ref[...]).astype(BF16)
-
-
-def expert(rows, gate, up, down):
+    o_ref[...] = dot_nt(hidden, w_ref[:, 2 * FFE :]).astype(BF16)
+
+
+def expert(rows, weights):
     return pl.pallas_call(
         expert_kernel,
         grid=(rows.shape[0] // EROWS,),
         out_shape=jax.ShapeDtypeStruct(rows.shape, BF16),
         in_specs=[
             pl.BlockSpec((EROWS, D), lambda i: (i, 0)),
-            pl.BlockSpec((D, FFE), lambda i: (0, 0)),
-            pl.BlockSpec((D, FFE), lambda i: (0, 0)),
-            pl.BlockSpec((FFE, D), lambda i: (0, 0)),
+            pl.BlockSpec((D, 3 * FFE), lambda i: (0, 0)),
         ],
         out_specs=pl.BlockSpec((EROWS, D), lambda i: (i, 0)),
         compiler_params=pltpu.CompilerParams(vmem_limit_bytes=48 * MIB),
         name="expert",
-    )(rows, gate, up, down)
+    )(rows, weights)
 
 
 CCOLS = 512
@@ -316,6 +325,15 @@
 
 
 DROWS = KVH * 8
+
+
+def pieces_of(x, count):
+    pieces = []
+    for _ in range(count):
+        piece = x.astype(BF16).astype(F32)
+        pieces.append(piece)
+        x = x - piece
+    return pieces
 
 
 def decode_kernel(info_ref, q_ref, kn_ref, vn_ref, k_ref, v_ref, o_ref):
@@ -336,6 +354,12 @@
     total = jnp.sum(weights, axis=1, keepdims=True) + fresh_weight
     fresh_round = fresh_weight.astype(BF16).astype(F32)
     weighted = dot_nn(weights.astype(BF16), v_ref[0]) + fresh_round * vn_ref[0].astype(F32)
+    weighted = weighted / jnp.maximum(total, 1e-30)
+    stats = pieces_of(top, 3) + pieces_of(total, 3)
+    lane = lax.broadcasted_iota(jnp.int32, (DROWS, 128), 1)
+    packed = jnp.zeros((DROWS, 128), F32)
+    for number, piece in enumerate(stats):
+        packed = jnp.where(lane >= HD + 8 * number, piece, packed)
     lane = lax.broadcasted_iota(jnp.int32, (8, 128), 1)
     for kv in range(KVH):
         rows = slice(8 * kv, 8 * kv + 8)
@@ -343,15 +367,14 @@
         piece = weighted[rows, lanes]
         if kv % 2:
             piece = swap_halves(piece)
-        piece = jnp.where(lane < HD, piece, jnp.where(lane < 96, top[rows], total[rows]))
-        o_ref[kv] = piece
+        o_ref[kv] = jnp.where(lane < HD, piece, packed[rows]).astype(BF16)
 
 
 def decode(info, query, key_new, value_new, key_cache, value_cache):
     return pl.pallas_call(
         decode_kernel,
         grid=(RLOC,),
-        out_shape=jax.ShapeDtypeStruct((SEQ, 8, 128), F32),
+        out_shape=jax.ShapeDtypeStruct((SEQ, 8, 128), BF16),
         in_specs=[
             pl.BlockSpec(memory_space=pltpu.SMEM),
             pl.BlockSpec((1, DROWS, KVH * HD), lambda i: (i, 0, 0)),
@@ -370,18 +393,24 @@
     return lax.all_to_all(x, "seq", split_axis=0, concat_axis=0, tiled=True)
 
 
-def gather_req(shard, axis):
+def join_req(own, pair, far, far_pair):
     index = lax.axis_index("req")
-    across = lax.ppermute(shard, "req", [(i, i ^ 2) for i in range(4)])
-    own_pair = lax.ppermute(shard, "req", [(i, i ^ 1) for i in range(4)])
-    far_pair = lax.ppermute(across, "req", [(i, i ^ 1) for i in range(4)])
-    size = shard.shape[axis]
-    shape = list(shard.shape)
-    shape[axis] = 4 * size
-    full = jnp.zeros(shape, shard.dtype)
-    for piece, flip in ((shard, 0), (own_pair, 1), (across, 2), (far_pair, 3)):
-        full = lax.dynamic_update_slice_in_dim(full, piece, (index ^ flip) * size, axis)
+    size = own.shape[0]
+    full = jnp.zeros((4 * size, own.shape[1]), own.dtype)
+    for piece, flip in ((own, 0), (pair, 1), (far, 2), (far_pair, 3)):
+        full = lax.dynamic_update_slice_in_dim(full, piece, (index ^ flip) * size, 0)
     return full
+
+
+def merge_decode(tails):
+    values = tails.astype(F32)
+    stats = values[:, :, HD : HD + 48].reshape(SEQ, 8, 6, 8)[..., 0]
+    tops = jnp.sum(stats[..., :3], axis=-1, keepdims=True)
+    totals = jnp.sum(stats[..., 3:], axis=-1, keepdims=True)
+    weights = totals * jnp.exp(tops - jnp.max(tops, axis=0, keepdims=True))
+    merged = jnp.sum(values[:, :, :HD] * weights, axis=0) / jnp.sum(weights, axis=0)
+    merged = jnp.pad(merged.astype(BF16), ((0, 0), (0, 128 - HD)))
+    return jnp.broadcast_to(merged[None], (SEQ, 8, 128))
 
 
 def block_query(dec_query):
@@ -413,11 +442,10 @@
 ):
     seq = lax.axis_index("seq").astype(jnp.int32)
     strip = (seq % PARTS).reshape(1)
+    own = jnp.concatenate([expert_gate[0], expert_up[0], expert_down[0].T], axis=1)
+    near = [(i, i ^ 1) for i in range(4)]
+    far = lax.ppermute(own, "req", [(i, i ^ 2) for i in range(4)])
     received = exchange(pack(prefill_query, prefill_key, prefill_value))
-    gate_up = jnp.concatenate([expert_gate[0], expert_up[0]], axis=1)
-    gate_up = gather_req(gate_up, 0)
-    gate, up = gate_up[:, :FFE], gate_up[:, FFE:]
-    down = gather_req(expert_down[0], 1)
     spread, matrix = route(routes, route_weights)
     info = jnp.concatenate([seq.reshape(1), cache_lengths])
     partial = decode(
@@ -428,24 +456,25 @@
         key_cache,
         value_cache,
     )
-    attended = exchange(attention(strip, received))
+    received, partial, spread, matrix = lax.optimization_barrier(
+        (received, partial, spread, matrix)
+    )
+    attended = exchange(attention(strip, received, partial))
+    attended, far = lax.optimization_barrier((attended, far))
     middle, outgoing = post(attended, attn_out_weight, prefill_resid, ffn_gain[None, :], spread)
+    outgoing, far, own = lax.optimization_barrier((outgoing, far, own))
     incoming = exchange(outgoing.reshape(EXPERTS, CAP, D)).reshape(SLOTS, D)
-    result = expert(incoming, gate, up, down)
+    weights = join_req(own, lax.ppermute(own, "req", near), far, lax.ppermute(far, "req", near))
+    incoming, weights = lax.optimization_barrier((incoming, weights))
+    result = expert(incoming, weights)
+    result, tails = lax.optimization_barrier((result, attended[:, QROWS:, :]))
     returned = exchange(result.reshape(EXPERTS, CAP, D)).reshape(SLOTS, D)
-    prefill_out = combine(matrix, returned, middle)
-
-    parts = exchange(partial)
-    tops = parts[..., HD : HD + 1]
-    top = jnp.max(tops, axis=0, keepdims=True)
-    merged = jnp.sum(parts * jnp.exp(tops - top), axis=0)
-    decoded = (merged[:, :HD] / merged[:, 96:97]).astype(BF16)
-    decoded = jnp.pad(decoded, ((0, 0), (0, 128 - HD)))
-    decoded = exchange(jnp.broadcast_to(decoded[None], (SEQ, 8, 128)))
+    decoded = exchange(merge_decode(tails))
     decoded = decoded[:, :GROUP, :HD].reshape(RLOC, HEADS * HD)
     dec_out = (
         dec_resid.astype(F32) + jnp.dot(decoded, attn_out_weight, preferred_element_type=F32)
     ).astype(BF16)
+    prefill_out = combine(matrix, returned, middle)
     return (prefill_out, dec_out)
 
 

time: 269 us -> 230 us (0.86)
  waiting for transfers between devices: 138 us -> 111 us
  starting transfers between devices: 52.1 us -> 26.4 us
  blocking collectives: 0 us -> 15.9 us
    ppermute x6 -> x3, waiting for transfers between devices: 58.1 us -> 0.01 us  [the longest x1 0.01 us: body(): lax.ppermute(own, 'req', near)]
    all_to_all x6 -> x4, waiting for transfers between devices: 79.4 us -> 111 us  [exchange(): return lax.all_to_all(x, 'seq', split_axis=0, concat_axis=0, tiled=True)]
    all_to_all x6 -> x4, starting transfers between devices: 49.3 us -> 24.8 us  [exchange(): return lax.all_to_all(x, 'seq', split_axis=0, concat_axis=0, tiled=True)]
    all_to_all x0 -> x1, blocking collectives: none -> 15.9 us  [exchange(): return lax.all_to_all(x, 'seq', split_axis=0, concat_axis=0, tiled=True)]
    unnamed x34 -> x39, local copies, waits for them, and re-layouts: 7.1 us -> 9.16 us
    dynamic_update_slice x7 -> x4, local copies, waits for them, and re-layouts: 8.37 us -> 8.28 us  [join_req(): lax.dynamic_update_slice_in_dim(full, piece, (index ^ flip) * size, 0)]
  transfers between devices with their start and end apart: 12 -> 7, of which waited for: 5 -> 4; matrix products, arithmetic and copies ran while one was open for 8% -> 7% of each run, Pallas kernels for 8% -> 12%
where the time goes in v2:
time: 230 us; the launch traced here: 229 us
  waiting for transfers between devices  111 us (48%)
  Pallas kernels  48.6 us (21%)
  starting transfers between devices  26.4 us (11%)
  local copies, waits for them, and re-layouts  21.1 us (9%)
  blocking collectives  15.9 us (7%)
  matrix products  3.66 us (2%)
    all_to_all x4, waiting for transfers between devices, exchange(): return lax.all_to_all(x, 'seq', split_axis=0, concat_axis=0, tiled=True)  111 us
    all_to_all x4, starting transfers between devices, exchange(): return lax.all_to_all(x, 'seq', split_axis=0, concat_axis=0, tiled=True)  24.8 us
    pallas_call x1, Pallas kernels, attention(): pl.pallas_call(attention_kernel, out_shape=jax.ShapeDtypeStruct((SEQ, BAC...  21.1 us
    all_to_all x1, blocking collectives, exchange(): return lax.all_to_all(x, 'seq', split_axis=0, concat_axis=0, tiled=True)  15.9 us
    pallas_call x1, Pallas kernels, expert(): pl.pallas_call(expert_kernel, grid=(rows.shape[0] // EROWS,), out_shape=j...  10 us
    unnamed x39, local copies, waits for them, and re-layouts  9.16 us
    dynamic_update_slice x4, local copies, waits for them, and re-layouts, join_req(): lax.dynamic_update_slice_in_dim(full, piece, (index ^ flip) * size, 0)  8.28 us
    pallas_call x1, Pallas kernels, decode(): pl.pallas_call(decode_kernel, grid=(RLOC,), out_shape=jax.ShapeDtypeStruc...  5.2 us
  transfers between devices with their start and end apart: 7, of which 4 were waited for; matrix products, arithmetic and copies ran while one was open for 7% of the time, Pallas kernels for 12%

profile of v2, /device:TPU:0, one launch (start us, length us, event | category | flops | bytes accessed | tf_op | source)
XLA Modules:
  0.0 229.1 jit_solution(1200618405484209181)
XLA Ops:
  0.6 1.0 copy-done.3
  1.6 0.9 copy-done.5
  2.5 0.9 copy-done.6
  3.4 2.0 pack.1
  5.5 10.9 %all-to-all-start = ((bf16[32,176,128]{2,1,0:T(8,128)(2,1)}), bf16[32,176,128]{2,1,0:T(8,128)(2,1)S(1)}, u32[]{:S(2)}, u32[]{:S(2)}) async-start(bf16[32,176,128]{2,1,0:T(8,128)(2,1)} %pack.1), calls=%async_computation | async-start | bytes 2883584 | tf_op jit(solution)/shard_map/all_to_all | solution.py:393
  16.4 0.2 copy.34
  16.6 1.1 pad_maximum_fusion
  17.7 1.0 collective-permute-start
  18.7 0.1 reshape.81
  18.8 0.1 mul.49
  19.0 0.3 mul.50
  19.3 0.1 mul.51
  19.4 0.1 mul.52
  19.6 0.1 copy.32.routes_ref
  19.7 0.1 copy.33.weights_ref
  19.8 1.0 route.1
  20.8 0.1 pad_add_fusion.info_ref
  20.9 2.2 copy-done.1
  23.1 5.2 %decode.1.dec_ref = bf16[32,8,128]{2,1,0:T(8,128)(2,1)S(1)} custom-call(s32[5]{0:T(128)S(1)} %pad_add_fusion.info_ref, bf16[4,64,512]{2,1,0:T(8,128)(2,1)S(1)} %broadcast_multiply_fusion.q_ref, bf16[4,1,512]{2,1,0:T(2,128)(2,1)S(1)} %copy.30.kn_ref, bf16[4,1,512]{2,1,0:T(2,128)(2,1)S(1)} %copy.31.vn_ref, bf16[4,1024,512]{2,1,0:T(8,128)(2,1)S(1)} %copy-done.1, ...), custom_call_target="tpu_custom_call" | custom-call | tf_op jit(solution)/shard_map/decode/pallas_call | solution.py:374
  28.3 11.7 %all-to-all-done.x_ref = bf16[32,176,128]{2,1,0:T(8,128)(2,1)S(1)} async-done(((bf16[32,176,128]{2,1,0:T(8,128)(2,1)}), bf16[32,176,128]{2,1,0:T(8,128)(2,1)S(1)}, u32[]{:S(2)}, u32[]{:S(2)}) %all-to-all-start) | async-done | bytes 1441824 | tf_op jit(solution)/shard_map/all_to_all | solution.py:393
  40.0 21.1 %attention.1 = bf16[32,56,128]{2,1,0:T(8,128)(2,1)} custom-call(s32[1]{0:T(128)} %bitcast.4.strip_ref, bf16[32,176,128]{2,1,0:T(8,128)(2,1)S(1)} %all-to-all-done.x_ref, bf16[32,8,128]{2,1,0:T(8,128)(2,1)S(1)} %decode.1.dec_ref), custom_call_target="tpu_custom_call" | custom-call | tf_op jit(solution)/shard_map/attention/pallas_call | solution.py:154
  61.1 4.1 %all-to-all-start.1 = ((bf16[32,56,128]{2,1,0:T(8,128)(2,1)}), bf16[32,56,128]{2,1,0:T(8,128)(2,1)S(1)}, u32[]{:S(2)}, u32[]{:S(2)}) async-start(bf16[32,56,128]{2,1,0:T(8,128)(2,1)} %attention.1), calls=%async_computation.1 | async-start | bytes 917504 | tf_op jit(solution)/shard_map/all_to_all | solution.py:393
  65.2 11.9 %all-to-all-done.1.x_ref = bf16[32,56,128]{2,1,0:T(8,128)(2,1)S(1)} async-done(((bf16[32,56,128]{2,1,0:T(8,128)(2,1)}), bf16[32,56,128]{2,1,0:T(8,128)(2,1)S(1)}, u32[]{:S(2)}, u32[]{:S(2)}) %all-to-all-start.1) | async-done | bytes 458784 | tf_op jit(solution)/shard_map/all_to_all | solution.py:393
  77.2 5.0 %post.1 = (bf16[128,1536]{1,0:T(8,128)(2,1)S(1)}, bf16[1280,1536]{1,0:T(8,128)(2,1)S(1)}) custom-call(bf16[32,56,128]{2,1,0:T(8,128)(2,1)S(1)} %all-to-all-done.1.x_ref, bf16[1536,1536]{1,0:T(8,128)(2,1)} %w_ref.1, bf16[128,1536]{1,0:T(8,128)(2,1)S(1)} %copy-done.4, f32[1,1536]{1,0:T(1,128)S(1)} %broadcast_in_dim.6.gain_ref, ...), custom_call_target="tpu_custom_call" | custom-call | tf_op jit(solution)/shard_map/post/pallas_call | solution.py:254
  82.2 1.9 copy-done.2
  84.1 4.9 %all-to-all-start.2 = ((bf16[32,40,1536]{2,1,0:T(8,128)(2,1)}), bf16[32,40,1536]{2,1,0:T(8,128)(2,1)}, u32[]{:S(2)}, u32[]{:S(2)}) async-start(bf16[32,40,1536]{2,1,0:T(8,128)(2,1)} %bitcast.25), calls=%async_computation.2 | async-start | bytes 7864320 | tf_op jit(solution)/shard_map/all_to_all | solution.py:393
  89.0 0.1 collective-permute-start.1
  89.0 0.5 collective-permute-start.2
  89.5 2.4 %broadcast_in_dim.7 = bf16[1536,1536]{1,0:T(8,128)(2,1)} broadcast(bf16[]{:T(256)} %constant.14.clone.1), dimensions={} | broadcast | bytes 4718594 | tf_op jit(solution)/shard_map/broadcast_in_dim | solution.py:399
  92.0 2.4 %constant_dynamic-update-slice_fusion.3 = bf16[1536,1536]{1,0:T(8,128)(2,1)} fusion(bf16[1536,1536]{1,0:T(8,128)(2,1)} %broadcast_in_dim.7, bf16[384,1536]{1,0:T(8,128)(2,1)} %pad_maximum_fusion, s32[]{:T(128)S(6)} %select_n.20), kind=kLoop, calls=%fused_computation.16 | loop fusion | bytes 2359300 | tf_op jit(solution)/shard_map/dynamic_update_slice | solution.py:401
  94.4 2.4 %constant_dynamic-update-slice_fusion.2 = bf16[1536,1536]{1,0:T(8,128)(2,1)} fusion(bf16[1536,1536]{1,0:T(8,128)(2,1)} %constant_dynamic-update-slice_fusion.3, bf16[384,1536]{1,0:T(8,128)(2,1)} %collective-permute-done.1, s32[]{:T(128)S(6)} %select_n.21), kind=kLoop, calls=%fused_computation.15 | loop fusion | bytes 2359300 | tf_op jit(solution)/shard_map/dynamic_update_slice | solution.py:401
  96.7 2.4 %constant_dynamic-update-slice_fusion.1 = bf16[1536,1536]{1,0:T(8,128)(2,1)} fusion(bf16[1536,1536]{1,0:T(8,128)(2,1)} %constant_dynamic-update-slice_fusion.2, bf16[384,1536]{1,0:T(8,128)(2,1)} %collective-permute-done, s32[]{:T(128)S(6)} %select_n.22), kind=kLoop, calls=%fused_computation.14 | loop fusion | bytes 2359300 | tf_op jit(solution)/shard_map/dynamic_update_slice | solution.py:401
  99.2 1.1 constant_dynamic-update-slice_fusion.w_ref
  100.3 39.6 %all-to-all-done.2 = bf16[32,40,1536]{2,1,0:T(8,128)(2,1)} async-done(((bf16[32,40,1536]{2,1,0:T(8,128)(2,1)}), bf16[32,40,1536]{2,1,0:T(8,128)(2,1)}, u32[]{:S(2)}, u32[]{:S(2)}) %all-to-all-start.2) | async-done | bytes 3932192 | tf_op jit(solution)/shard_map/all_to_all | solution.py:393
  139.8 10.0 %expert.1 = bf16[1280,1536]{1,0:T(8,128)(2,1)S(1)} custom-call(bf16[1280,1536]{1,0:T(8,128)(2,1)} %bitcast.10.x_ref, bf16[1536,1536]{1,0:T(8,128)(2,1)} %constant_dynamic-update-slice_fusion.w_ref), custom_call_target="tpu_custom_call" | custom-call | tf_op jit(solution)/shard_map/expert/pallas_call | solution.py:289
  149.9 1.9 copy-done
  151.7 0.1 slice.29
  151.8 0.1 copy.35
  152.0 0.1 reduce_max.9
  152.1 0.2 fusion.3
  152.3 0.1 copy.37
  152.4 0.1 fusion.1
  152.6 15.9 %all_to_all.25 = bf16[32,8,128]{2,1,0:T(8,128)(2,1)S(1)} all-to-all(bf16[32,8,128]{2,1,0:T(8,128)(2,1)S(1)} %broadcast_in_dim.8), channel_id=1, replica_groups=mesh['req'=4,'seq'=32] {'seq'}, dimensions={0} | all-to-all | bytes 131072 | tf_op jit(solution)/shard_map/all_to_all | solution.py:393
  168.5 5.0 %all-to-all-start.3 = ((bf16[32,40,1536]{2,1,0:T(8,128)(2,1)}), bf16[32,40,1536]{2,1,0:T(8,128)(2,1)}, u32[]{:S(2)}, u32[]{:S(2)}) async-start(bf16[32,40,1536]{2,1,0:T(8,128)(2,1)} %bitcast.24), calls=%async_computation.3 | async-start | bytes 7864320 | tf_op jit(solution)/shard_map/all_to_all | solution.py:393
  173.5 0.1 reshape.90
  173.6 3.7 %fusion = bf16[4,1536]{1,0:T(4,128)(2,1)} fusion(bf16[4,1536]{1,0:T(4,128)(2,1)S(1)} %reshape.90, bf16[1536,1536]{1,0:T(8,128)(2,1)} %w_ref.1, bf16[4,1536]{1,0:T(4,128)(2,1)S(1)} %copy-done.12), kind=kOutput, calls=%fused_computation.1 | convolution fusion | flops 18892800 | bytes 4755456 | tf_op jit(solution)/shard_map/dot_general | solution.py:475
  177.3 47.5 %all-to-all-done.3 = bf16[32,40,1536]{2,1,0:T(8,128)(2,1)} async-done(((bf16[32,40,1536]{2,1,0:T(8,128)(2,1)}), bf16[32,40,1536]{2,1,0:T(8,128)(2,1)}, u32[]{:S(2)}, u32[]{:S(2)}) %all-to-all-start.3) | async-done | bytes 3932192 | tf_op jit(solution)/shard_map/all_to_all | solution.py:393
  224.8 4.4 %combine.1 = bf16[128,1536]{1,0:T(8,128)(2,1)} custom-call(bf16[256,1280]{1,0:T(8,128)(2,1)S(1)} %get-tuple-element.21.c_ref, bf16[1280,1536]{1,0:T(8,128)(2,1)} %bitcast.12.x_ref, bf16[128,1536]{1,0:T(8,128)(2,1)S(1)} %get-tuple-element.34.mid_ref), custom_call_target="tpu_custom_call" | custom-call | tf_op jit(solution)/shard_map/combine/pallas_call | solution.py:312
  (48 shorter events, 0.3 us)
Async XLA Ops:
  0.6 1.0 copy-start.3
  1.6 0.9 copy-start.5
  2.5 0.9 copy-start.6
  3.4 12.9 %copy-start.10 = (bf16[1,512,384]{2,1,0:T(8,128)(2,1)S(1)}, bf16[1,512,384]{2,1,0:T(8,128)(2,1)}, u32[]{:S(2)}) copy-start(bf16[1,512,384]{2,1,0:T(8,128)(2,1)} %param.33) | copy-start | bytes 1179652
  3.4 13.1 %copy-start.8 = (bf16[1,384,512]{2,1,0:T(8,128)(2,1)S(1)}, bf16[1,384,512]{2,1,0:T(8,128)(2,1)}, u32[]{:S(2)}) copy-start(bf16[1,384,512]{2,1,0:T(8,128)(2,1)} %param.32) | copy-start | bytes 1179652
  3.4 13.1 %copy-start.9 = (bf16[1,384,512]{2,1,0:T(8,128)(2,1)S(1)}, bf16[1,384,512]{2,1,0:T(8,128)(2,1)}, u32[]{:S(2)}) copy-start(bf16[1,384,512]{2,1,0:T(8,128)(2,1)} %param.31) | copy-start | bytes 1179652
  3.4 15.3 %copy-start.11 = (bf16[4,1536]{1,0:T(4,128)(2,1)S(1)}, bf16[4,1536]{1,0:T(4,128)(2,1)}, u32[]{:S(2)}) copy-start(bf16[4,1536]{1,0:T(4,128)(2,1)} %param.22) | copy-start | bytes 36868
  5.5 14.1 %copy-start.14 = (bf16[4,512]{1,0:T(4,128)(2,1)S(1)}, bf16[4,512]{1,0:T(4,128)(2,1)}, u32[]{:S(2)}) copy-start(bf16[4,512]{1,0:T(4,128)(2,1)} %param.23) | copy-start | bytes 12292
  5.5 14.1 %copy-start.15 = (bf16[4,512]{1,0:T(4,128)(2,1)S(1)}, bf16[4,512]{1,0:T(4,128)(2,1)}, u32[]{:S(2)}) copy-start(bf16[4,512]{1,0:T(4,128)(2,1)} %param.24) | copy-start | bytes 12292
  5.5 14.1 %copy-start.7 = (s32[128,8]{0,1:T(8,128)S(1)}, s32[128,8]{0,1:T(8,128)}, u32[]{:S(2)}) copy-start(s32[128,8]{0,1:T(8,128)} %param.34) | copy-start | bytes 12292
  5.5 14.2 %copy-start.16 = (f32[128,8]{0,1:T(8,128)S(1)}, f32[128,8]{0,1:T(8,128)}, u32[]{:S(2)}) copy-start(f32[128,8]{0,1:T(8,128)} %param.35) | copy-start | bytes 12292
  5.5 15.3 %copy-start.17 = (s32[4]{0:T(128)S(1)}, s32[4]{0:T(128)}, u32[]{:S(2)}) copy-start(s32[4]{0:T(128)} %param.26) | copy-start | bytes 52
  5.5 34.5 %all-to-all-start = ((bf16[32,176,128]{2,1,0:T(8,128)(2,1)}), bf16[32,176,128]{2,1,0:T(8,128)(2,1)S(1)}, u32[]{:S(2)}, u32[]{:S(2)}) async-start(bf16[32,176,128]{2,1,0:T(8,128)(2,1)} %pack.1), calls=%async_computation | async-start | bytes 2883584 | tf_op jit(solution)/shard_map/all_to_all | solution.py:393
  17.7 47.5 %collective-permute-start = (bf16[384,1536]{1,0:T(8,128)(2,1)}, bf16[384,1536]{1,0:T(8,128)(2,1)}, u32[]{:S(2)}, u32[]{:S(2)}) collective-permute-start(bf16[384,1536]{1,0:T(8,128)(2,1)} %pad_maximum_fusion), channel_id=1, source_target_pairs={{0,64},{32,96},{64,0},{96,32},{1,65},{33,97},{65,1},{97,33},{2,66}... | collective-permute-start | bytes 3538952 | tf_op jit(solution)/shard_map/ppermute | solution.py:447
  20.9 2.2 copy-start.1
  23.1 42.1 %copy-start.13 = (f32[1536]{0:T(1024)S(1)}, f32[1536]{0:T(1024)}, u32[]{:S(2)}) copy-start(f32[1536]{0:T(1024)} %param.30) | copy-start | bytes 18436
  23.1 54.1 %copy-start.4 = (bf16[128,1536]{1,0:T(8,128)(2,1)S(1)}, bf16[128,1536]{1,0:T(8,128)(2,1)}, u32[]{:S(2)}) copy-start(bf16[128,1536]{1,0:T(8,128)(2,1)} %resid_ref.1) | copy-start | bytes 1179652
  61.1 16.1 %all-to-all-start.1 = ((bf16[32,56,128]{2,1,0:T(8,128)(2,1)}), bf16[32,56,128]{2,1,0:T(8,128)(2,1)S(1)}, u32[]{:S(2)}, u32[]{:S(2)}) async-start(bf16[32,56,128]{2,1,0:T(8,128)(2,1)} %attention.1), calls=%async_computation.1 | async-start | bytes 917504 | tf_op jit(solution)/shard_map/all_to_all | solution.py:393
  82.2 1.9 copy-start.2
  84.1 55.7 %all-to-all-start.2 = ((bf16[32,40,1536]{2,1,0:T(8,128)(2,1)}), bf16[32,40,1536]{2,1,0:T(8,128)(2,1)}, u32[]{:S(2)}, u32[]{:S(2)}) async-start(bf16[32,40,1536]{2,1,0:T(8,128)(2,1)} %bitcast.25), calls=%async_computation.2 | async-start | bytes 7864320 | tf_op jit(solution)/shard_map/all_to_all | solution.py:393
  89.0 5.4 %collective-permute-start.1 = (bf16[384,1536]{1,0:T(8,128)(2,1)}, bf16[384,1536]{1,0:T(8,128)(2,1)}, u32[]{:S(2)}, u32[]{:S(2)}) collective-permute-start(bf16[384,1536]{1,0:T(8,128)(2,1)} %pad_maximum_fusion), channel_id=1, source_target_pairs={{0,32},{32,0},{64,96},{96,64},{1,33},{33,1},{65,97},{97,65},{2,34}... | collective-permute-start | bytes 3538952 | tf_op jit(solution)/shard_map/ppermute | solution.py:467
  89.0 10.1 %collective-permute-start.2 = (bf16[384,1536]{1,0:T(8,128)(2,1)}, bf16[384,1536]{1,0:T(8,128)(2,1)S(1)}, u32[]{:S(2)}, u32[]{:S(2)}) collective-permute-start(bf16[384,1536]{1,0:T(8,128)(2,1)} %collective-permute-done), channel_id=1, source_target_pairs={{0,32},{32,0},{64,96},{96,64},{1,33},{33,1},{65,97},{97,65},{2,34}... | collective-permute-start | bytes 3538952 | tf_op jit(solution)/shard_map/ppermute | solution.py:467
  149.8 1.9 copy-start
  168.5 5.1 %copy-start.12 = (bf16[4,1536]{1,0:T(4,128)(2,1)S(1)}, bf16[4,1536]{1,0:T(4,128)(2,1)}, u32[]{:S(2)}) copy-start(bf16[4,1536]{1,0:T(4,128)(2,1)} %param.25) | copy-start | bytes 36868
  168.5 56.3 %all-to-all-start.3 = ((bf16[32,40,1536]{2,1,0:T(8,128)(2,1)}), bf16[32,40,1536]{2,1,0:T(8,128)(2,1)}, u32[]{:S(2)}, u32[]{:S(2)}) async-start(bf16[32,40,1536]{2,1,0:T(8,128)(2,1)} %bitcast.24), calls=%async_computation.3 | async-start | bytes 7864320 | tf_op jit(solution)/shard_map/all_to_all | solution.py:393

commit v3 on v2

--- a/solution.py
+++ b/solution.py
@@ -39,6 +39,10 @@
 
 def left_lanes(shape):
     return lax.broadcasted_iota(jnp.int32, shape, len(shape) - 1) < HD
+
+
+def in_hbm(x):
+    return pltpu.with_memory_space_constraint(x, pltpu.HBM)
 
 
 def dot_nt(a, b):
@@ -81,7 +85,7 @@
     return pl.pallas_call(
         pack_kernel,
         grid=(PACK_STEPS,),
-        out_shape=jax.ShapeDtypeStruct((SEQ, PACK, 128), BF16),
+        out_shape=pltpu.HBM((SEQ, PACK, 128), BF16),
         in_specs=[
             pl.BlockSpec((TOK, PAIRS * 128), lambda i: (0, i)),
             pl.BlockSpec((TOK, 128), lambda i: (0, i)),
@@ -90,7 +94,7 @@
         out_specs=pl.BlockSpec((SEQ // PACK_STEPS, PACK, 128), lambda i: (i, 0, 0)),
         compiler_params=pltpu.CompilerParams(vmem_limit_bytes=32 * MIB),
         name="pack",
-    )(query, key, value)
+    )(in_hbm(query), in_hbm(key), in_hbm(value))
 
 
 QS = 8
@@ -256,7 +260,7 @@
         grid=(steps,),
         out_shape=(
             jax.ShapeDtypeStruct((TOK, D), BF16),
-            jax.ShapeDtypeStruct((SLOTS, D), BF16),
+            pltpu.HBM((SLOTS, D), BF16),
         ),
         in_specs=[
             pl.BlockSpec((SEQ, BACK, 128), lambda i: (0, 0, 0)),
@@ -289,7 +293,7 @@
     return pl.pallas_call(
         expert_kernel,
         grid=(rows.shape[0] // EROWS,),
-        out_shape=jax.ShapeDtypeStruct(rows.shape, BF16),
+        out_shape=pltpu.HBM(rows.shape, BF16),
         in_specs=[
             pl.BlockSpec((EROWS, D), lambda i: (i, 0)),
             pl.BlockSpec((D, 3 * FFE), lambda i: (0, 0)),
@@ -393,6 +397,18 @@
     return lax.all_to_all(x, "seq", split_axis=0, concat_axis=0, tiled=True)
 
 
+def gather_seq(tile):
+    seq = lax.axis_index("seq")
+    tiles = tile[None]
+    for step in (1, 2, 4, 8, 16):
+        other = lax.ppermute(tiles, "seq", [(i, i ^ step) for i in range(SEQ)])
+        upper = (seq & step) != 0
+        tiles = jnp.concatenate(
+            [jnp.where(upper, other, tiles), jnp.where(upper, tiles, other)], axis=0
+        )
+    return tiles
+
+
 def join_req(own, pair, far, far_pair):
     index = lax.axis_index("req")
     size = own.shape[0]
@@ -409,8 +425,7 @@
     totals = jnp.sum(stats[..., 3:], axis=-1, keepdims=True)
     weights = totals * jnp.exp(tops - jnp.max(tops, axis=0, keepdims=True))
     merged = jnp.sum(values[:, :, :HD] * weights, axis=0) / jnp.sum(weights, axis=0)
-    merged = jnp.pad(merged.astype(BF16), ((0, 0), (0, 128 - HD)))
-    return jnp.broadcast_to(merged[None], (SEQ, 8, 128))
+    return jnp.pad(merged.astype(BF16), ((0, 0), (0, 128 - HD)))
 
 
 def block_query(dec_query):
@@ -462,14 +477,15 @@
     attended = exchange(attention(strip, received, partial))
     attended, far = lax.optimization_barrier((attended, far))
     middle, outgoing = post(attended, attn_out_weight, prefill_resid, ffn_gain[None, :], spread)
-    outgoing, far, own = lax.optimization_barrier((outgoing, far, own))
+    outgoing, far, own, tails = lax.optimization_barrier(
+        (outgoing, far, own, attended[:, QROWS:, :])
+    )
     incoming = exchange(outgoing.reshape(EXPERTS, CAP, D)).reshape(SLOTS, D)
     weights = join_req(own, lax.ppermute(own, "req", near), far, lax.ppermute(far, "req", near))
+    decoded = gather_seq(merge_decode(tails))
     incoming, weights = lax.optimization_barrier((incoming, weights))
     result = expert(incoming, weights)
-    result, tails = lax.optimization_barrier((result, attended[:, QROWS:, :]))
     returned = exchange(result.reshape(EXPERTS, CAP, D)).reshape(SLOTS, D)
-    decoded = exchange(merge_decode(tails))
     decoded = decoded[:, :GROUP, :HD].reshape(RLOC, HEADS * HD)
     dec_out = (
         dec_resid.astype(F32) + jnp.dot(decoded, attn_out_weight, preferred_element_type=F32)

time: 230 us -> 227 us (0.987)
  starting transfers between devices: 26.4 us -> 50.5 us
  blocking collectives: 15.9 us -> 0 us
  waiting for transfers between devices: 111 us -> 101 us
  local copies, waits for them, and re-layouts: 21.1 us -> 14.2 us
  Pallas kernels: 48.6 us -> 52.7 us
    all_to_all x4, waiting for transfers between devices: 111 us -> 63.7 us  [exchange(): return lax.all_to_all(x, 'seq', split_axis=0, concat_axis=0, tiled=True)]
    ppermute x0 -> x5, waiting for transfers between devices: none -> 37.6 us  [gather_seq(): other = lax.ppermute(tiles, 'seq', [(i, i ^ step) for i in range(SEQ)])]
    ppermute x0 -> x5, starting transfers between devices: none -> 22.5 us  [gather_seq(): other = lax.ppermute(tiles, 'seq', [(i, i ^ step) for i in range(SEQ)])]
    all_to_all x1 -> x0, blocking collectives: 15.9 us -> none  [exchange(): return lax.all_to_all(x, 'seq', split_axis=0, concat_axis=0, tiled=True)]
    unnamed x39 -> x27, local copies, waits for them, and re-layouts: 9.16 us -> 3.6 us
    pallas_call x2, Pallas kernels: 12 us -> 14.6 us  [the longest x1 10.9 us: expert(): pl.pallas_call(expert_kernel, grid=(rows.shape[0] // EROWS,), out_shape=p...]
  transfers between devices with their start and end apart: 7 -> 12, of which waited for: 4 -> 8; matrix products, arithmetic and copies ran while one was open for 7% -> 8% of each run, Pallas kernels for 12% -> 12%
where the time goes in v3:
time: 227 us; the launch traced here: 225 us
  waiting for transfers between devices  101 us (44%)
  Pallas kernels  52.7 us (23%)
  starting transfers between devices  50.5 us (22%)
  local copies, waits for them, and re-layouts  14.2 us (6%)
  matrix products  3.66 us (2%)
    all_to_all x4, waiting for transfers between devices, exchange(): return lax.all_to_all(x, 'seq', split_axis=0, concat_axis=0, tiled=True)  63.7 us
    ppermute x5, waiting for transfers between devices, gather_seq(): other = lax.ppermute(tiles, 'seq', [(i, i ^ step) for i in range(SEQ)])  37.6 us
    all_to_all x4, starting transfers between devices, exchange(): return lax.all_to_all(x, 'seq', split_axis=0, concat_axis=0, tiled=True)  26.4 us
    ppermute x5, starting transfers between devices, gather_seq(): other = lax.ppermute(tiles, 'seq', [(i, i ^ step) for i in range(SEQ)])  22.5 us
    pallas_call x1, Pallas kernels, attention(): pl.pallas_call(attention_kernel, out_shape=jax.ShapeDtypeStruct((SEQ, BAC...  21.1 us
    pallas_call x1, Pallas kernels, expert(): pl.pallas_call(expert_kernel, grid=(rows.shape[0] // EROWS,), out_shape=p...  10.9 us
    dynamic_update_slice x4, local copies, waits for them, and re-layouts, join_req(): lax.dynamic_update_slice_in_dim(full, piece, (index ^ flip) * size, 0)  6.96 us
    pallas_call x1, Pallas kernels, post(): pl.pallas_call(post_kernel, grid=(steps,), out_shape=(jax.ShapeDtypeStruc...  6.56 us
  transfers between devices with their start and end apart: 12, of which 8 were waited for; matrix products, arithmetic and copies ran while one was open for 8% of the time, Pallas kernels for 12%

profile of v3, /device:TPU:0, one launch (start us, length us, event | category | flops | bytes accessed | tf_op | source)
XLA Modules:
  0.0 225.1 jit_solution(6748388510677605435)
XLA Ops:
  0.7 3.7 %pack.1 = bf16[32,176,128]{2,1,0:T(8,128)(2,1)} custom-call(bf16[128,1536]{1,0:T(8,128)(2,1)} %q_ref.1, bf16[128,512]{1,0:T(8,128)(2,1)} %k_ref.2, bf16[128,512]{1,0:T(8,128)(2,1)} %v_ref.2), custom_call_target="tpu_custom_call" | custom-call | tf_op jit(solution)/shard_map/pack/pallas_call | solution.py:85
  4.4 10.9 %all-to-all-start = ((bf16[32,176,128]{2,1,0:T(8,128)(2,1)}), bf16[32,176,128]{2,1,0:T(8,128)(2,1)S(1)}, u32[]{:S(2)}, u32[]{:S(2)}) async-start(bf16[32,176,128]{2,1,0:T(8,128)(2,1)} %pack.1), calls=%async_computation | async-start | bytes 2883584 | tf_op jit(solution)/shard_map/all_to_all | solution.py:397
  15.2 1.2 copy.34
  16.4 1.1 pad_maximum_fusion
  17.5 1.0 collective-permute-start
  18.5 0.1 reshape.80
  18.7 0.1 mul.49
  18.8 0.3 mul.50
  19.1 0.1 mul.51
  19.2 0.1 mul.52
  19.4 0.1 copy.32.routes_ref
  19.5 0.1 copy.33.weights_ref
  19.6 1.0 route.1
  20.7 2.2 copy-done
  22.9 5.2 %decode.1.dec_ref = bf16[32,8,128]{2,1,0:T(8,128)(2,1)S(1)} custom-call(s32[5]{0:T(128)S(1)} %pad_add_fusion.info_ref, bf16[4,64,512]{2,1,0:T(8,128)(2,1)S(1)} %broadcast_multiply_fusion.q_ref, bf16[4,1,512]{2,1,0:T(2,128)(2,1)S(1)} %copy.30.kn_ref, bf16[4,1,512]{2,1,0:T(2,128)(2,1)S(1)} %copy.31.vn_ref, bf16[4,1024,512]{2,1,0:T(8,128)(2,1)S(1)} %copy-done, ...), custom_call_target="tpu_custom_call" | custom-call | tf_op jit(solution)/shard_map/decode/pallas_call | solution.py:378
  28.1 10.8 %all-to-all-done.x_ref = bf16[32,176,128]{2,1,0:T(8,128)(2,1)S(1)} async-done(((bf16[32,176,128]{2,1,0:T(8,128)(2,1)}), bf16[32,176,128]{2,1,0:T(8,128)(2,1)S(1)}, u32[]{:S(2)}, u32[]{:S(2)}) %all-to-all-start) | async-done | bytes 1441824 | tf_op jit(solution)/shard_map/all_to_all | solution.py:397
  38.9 21.1 %attention.1 = bf16[32,56,128]{2,1,0:T(8,128)(2,1)} custom-call(s32[1]{0:T(128)} %bitcast.4.strip_ref, bf16[32,176,128]{2,1,0:T(8,128)(2,1)S(1)} %all-to-all-done.x_ref, bf16[32,8,128]{2,1,0:T(8,128)(2,1)S(1)} %decode.1.dec_ref), custom_call_target="tpu_custom_call" | custom-call | tf_op jit(solution)/shard_map/attention/pallas_call | solution.py:158
  60.0 4.1 %all-to-all-start.1 = ((bf16[32,56,128]{2,1,0:T(8,128)(2,1)}), bf16[32,56,128]{2,1,0:T(8,128)(2,1)S(1)}, u32[]{:S(2)}, u32[]{:S(2)}) async-start(bf16[32,56,128]{2,1,0:T(8,128)(2,1)} %attention.1), calls=%async_computation.1 | async-start | bytes 917504 | tf_op jit(solution)/shard_map/all_to_all | solution.py:397
  64.1 11.9 %all-to-all-done.1.x_ref = bf16[32,56,128]{2,1,0:T(8,128)(2,1)S(1)} async-done(((bf16[32,56,128]{2,1,0:T(8,128)(2,1)}), bf16[32,56,128]{2,1,0:T(8,128)(2,1)S(1)}, u32[]{:S(2)}, u32[]{:S(2)}) %all-to-all-start.1) | async-done | bytes 458784 | tf_op jit(solution)/shard_map/all_to_all | solution.py:397
  76.1 6.6 %post.1 = (bf16[128,1536]{1,0:T(8,128)(2,1)S(1)}, bf16[1280,1536]{1,0:T(8,128)(2,1)}) custom-call(bf16[32,56,128]{2,1,0:T(8,128)(2,1)S(1)} %all-to-all-done.1.x_ref, bf16[1536,1536]{1,0:T(8,128)(2,1)} %w_ref.1, bf16[128,1536]{1,0:T(8,128)(2,1)S(1)} %copy-done.1, f32[1,1536]{1,0:T(1,128)S(1)} %broadcast_in_dim.6.gain_ref, ...), custom_call_target="tpu_custom_call" | custom-call | tf_op jit(solution)/shard_map/post/pallas_call | solution.py:258
  82.6 4.8 %all-to-all-start.2 = ((bf16[32,40,1536]{2,1,0:T(8,128)(2,1)}), bf16[32,40,1536]{2,1,0:T(8,128)(2,1)}, u32[]{:S(2)}, u32[]{:S(2)}) async-start(bf16[32,40,1536]{2,1,0:T(8,128)(2,1)} %bitcast.32), calls=%async_computation.2 | async-start | bytes 7864320 | tf_op jit(solution)/shard_map/all_to_all | solution.py:397
  87.5 0.1 collective-permute-start.1
  87.6 0.5 collective-permute-start.2
  88.1 2.5 %broadcast_in_dim.7 = bf16[1536,1536]{1,0:T(8,128)(2,1)} broadcast(bf16[]{:T(256)} %constant.16.clone.1), dimensions={} | broadcast | bytes 4718594 | tf_op jit(solution)/shard_map/broadcast_in_dim | solution.py:415
  90.5 2.4 %constant_dynamic-update-slice_fusion.3 = bf16[1536,1536]{1,0:T(8,128)(2,1)} fusion(bf16[1536,1536]{1,0:T(8,128)(2,1)} %broadcast_in_dim.7, bf16[384,1536]{1,0:T(8,128)(2,1)} %pad_maximum_fusion, s32[]{:T(128)S(6)} %select_n.80), kind=kLoop, calls=%fused_computation.32 | loop fusion | bytes 2359300 | tf_op jit(solution)/shard_map/dynamic_update_slice | solution.py:417
  92.9 1.1 constant_dynamic-update-slice_fusion.2
  94.0 2.4 %constant_dynamic-update-slice_fusion.1 = bf16[1536,1536]{1,0:T(8,128)(2,1)} fusion(bf16[1536,1536]{1,0:T(8,128)(2,1)} %constant_dynamic-update-slice_fusion.2, bf16[384,1536]{1,0:T(8,128)(2,1)} %collective-permute-done, s32[]{:T(128)S(6)} %select_n.82), kind=kLoop, calls=%fused_computation.30 | loop fusion | bytes 2359300 | tf_op jit(solution)/shard_map/dynamic_update_slice | solution.py:417
  96.4 1.1 constant_dynamic-update-slice_fusion.w_ref
  97.5 41.0 %all-to-all-done.2 = bf16[32,40,1536]{2,1,0:T(8,128)(2,1)} async-done(((bf16[32,40,1536]{2,1,0:T(8,128)(2,1)}), bf16[32,40,1536]{2,1,0:T(8,128)(2,1)}, u32[]{:S(2)}, u32[]{:S(2)}) %all-to-all-start.2) | async-done | bytes 3932192 | tf_op jit(solution)/shard_map/all_to_all | solution.py:397
  138.5 10.9 %expert.1 = bf16[1280,1536]{1,0:T(8,128)(2,1)} custom-call(bf16[1280,1536]{1,0:T(8,128)(2,1)} %bitcast.10.x_ref, bf16[1536,1536]{1,0:T(8,128)(2,1)} %constant_dynamic-update-slice_fusion.w_ref), custom_call_target="tpu_custom_call" | custom-call | tf_op jit(solution)/shard_map/expert/pallas_call | solution.py:293
  149.4 6.5 %all-to-all-start.3 = ((bf16[32,40,1536]{2,1,0:T(8,128)(2,1)}), bf16[32,40,1536]{2,1,0:T(8,128)(2,1)}, u32[]{:S(2)}, u32[]{:S(2)}) async-start(bf16[32,40,1536]{2,1,0:T(8,128)(2,1)} %bitcast.31), calls=%async_computation.3 | async-start | bytes 7864320 | tf_op jit(solution)/shard_map/all_to_all | solution.py:397
  155.9 0.1 slice.29
  156.0 0.1 copy.35
  156.2 0.1 reduce_max.9
  156.3 0.2 fusion.3
  156.6 0.1 fusion.1
  156.8 3.3 %collective-permute-start.3 = (bf16[1,8,128]{2,1,0:T(8,128)(2,1)S(1)}, bf16[1,8,128]{2,1,0:T(8,128)(2,1)S(1)}, u32[]{:S(2)}, u32[]{:S(2)}) collective-permute-start(bf16[1,8,128]{2,1,0:T(8,128)(2,1)S(1)} %pad_bitcast_fusion), channel_id=1, source_target_pairs={{0,1},{1,0},{2,3},{3,2},{4,5},{5,4},{6,7},{7,6},{8,9},{9,8},{10,11... | collective-permute-start | bytes 6152 | tf_op jit(solution)/shard_map/ppermute | solution.py:404
  160.1 23.3 %collective-permute-done.3 = bf16[1,8,128]{2,1,0:T(8,128)(2,1)S(1)} collective-permute-done((bf16[1,8,128]{2,1,0:T(8,128)(2,1)S(1)}, bf16[1,8,128]{2,1,0:T(8,128)(2,1)S(1)}, u32[]{:S(2)}, u32[]{:S(2)}) %collective-permute-start.3) | collective-permute-done | bytes 2080 | tf_op jit(solution)/shard_map/ppermute | solution.py:404
  183.4 10.9 %collective-permute-start.4 = (bf16[2,8,128]{2,1,0:T(8,128)(2,1)S(1)}, bf16[2,8,128]{2,1,0:T(8,128)(2,1)S(1)}, u32[]{:S(2)}, u32[]{:S(2)}) collective-permute-start(bf16[2,8,128]{2,1,0:T(8,128)(2,1)S(1)} %pad_maximum_fusion.5), channel_id=1, source_target_pairs={{0,2},{1,3},{2,0},{3,1},{4,6},{5,7},{6,4},{7,5},{8,10},{9,11},{10,... | collective-permute-start | bytes 12296 | tf_op jit(solution)/shard_map/ppermute | solution.py:404
  194.3 5.5 %collective-permute-done.4 = bf16[2,8,128]{2,1,0:T(8,128)(2,1)S(1)} collective-permute-done((bf16[2,8,128]{2,1,0:T(8,128)(2,1)S(1)}, bf16[2,8,128]{2,1,0:T(8,128)(2,1)S(1)}, u32[]{:S(2)}, u32[]{:S(2)}) %collective-permute-start.4) | collective-permute-done | bytes 4128 | tf_op jit(solution)/shard_map/ppermute | solution.py:404
  199.8 6.1 %collective-permute-start.5 = (bf16[4,8,128]{2,1,0:T(8,128)(2,1)S(1)}, bf16[4,8,128]{2,1,0:T(8,128)(2,1)S(1)}, u32[]{:S(2)}, u32[]{:S(2)}) collective-permute-start(bf16[4,8,128]{2,1,0:T(8,128)(2,1)S(1)} %pad_maximum_fusion.4), channel_id=1, source_target_pairs={{0,4},{1,5},{2,6},{3,7},{4,0},{5,1},{6,2},{7,3},{8,12},{9,13},{10,... | collective-permute-start | bytes 24584 | tf_op jit(solution)/shard_map/ppermute | solution.py:404
  206.0 1.6 collective-permute-done.5
  207.7 3.7 %collective-permute-done.6 = bf16[8,8,128]{2,1,0:T(8,128)(2,1)S(1)} collective-permute-done((bf16[8,8,128]{2,1,0:T(8,128)(2,1)S(1)}, bf16[8,8,128]{2,1,0:T(8,128)(2,1)S(1)}, u32[]{:S(2)}, u32[]{:S(2)}) %collective-permute-start.6) | collective-permute-done | bytes 16416 | tf_op jit(solution)/shard_map/ppermute | solution.py:404
  211.4 2.1 collective-permute-start.7
  213.6 3.4 %collective-permute-done.7 = bf16[16,8,128]{2,1,0:T(8,128)(2,1)S(1)} collective-permute-done((bf16[16,8,128]{2,1,0:T(8,128)(2,1)S(1)}, bf16[16,8,128]{2,1,0:T(8,128)(2,1)S(1)}, u32[]{:S(2)}, u32[]{:S(2)}) %collective-permute-start.7) | collective-permute-done | bytes 32800 | tf_op jit(solution)/shard_map/ppermute | solution.py:404
  217.0 0.1 reshape.89
  217.1 3.7 %fusion = bf16[4,1536]{1,0:T(4,128)(2,1)} fusion(bf16[4,1536]{1,0:T(4,128)(2,1)S(1)} %reshape.89, bf16[1536,1536]{1,0:T(8,128)(2,1)} %w_ref.1, bf16[4,1536]{1,0:T(4,128)(2,1)S(1)} %copy-done.6), kind=kOutput, calls=%fused_computation.1 | convolution fusion | flops 18892800 | bytes 4755456 | tf_op jit(solution)/shard_map/dot_general | solution.py:491
  220.7 4.4 %combine.1 = bf16[128,1536]{1,0:T(8,128)(2,1)} custom-call(bf16[256,1280]{1,0:T(8,128)(2,1)S(1)} %get-tuple-element.20.c_ref, bf16[1280,1536]{1,0:T(8,128)(2,1)} %bitcast.12.x_ref, bf16[128,1536]{1,0:T(8,128)(2,1)S(1)} %get-tuple-element.32.mid_ref), custom_call_target="tpu_custom_call" | custom-call | tf_op jit(solution)/shard_map/combine/pallas_call | solution.py:316
  (53 shorter events, 0.6 us)
Async XLA Ops:
  0.6 15.8 %copy-start.4 = (bf16[1,384,512]{2,1,0:T(8,128)(2,1)S(1)}, bf16[1,384,512]{2,1,0:T(8,128)(2,1)}, u32[]{:S(2)}) copy-start(bf16[1,384,512]{2,1,0:T(8,128)(2,1)} %param.31) | copy-start | bytes 1179652
  0.6 15.8 %copy-start.3 = (bf16[1,384,512]{2,1,0:T(8,128)(2,1)S(1)}, bf16[1,384,512]{2,1,0:T(8,128)(2,1)}, u32[]{:S(2)}) copy-start(bf16[1,384,512]{2,1,0:T(8,128)(2,1)} %param.32) | copy-start | bytes 1179652
  0.7 17.9 %copy-start.5 = (bf16[4,1536]{1,0:T(4,128)(2,1)S(1)}, bf16[4,1536]{1,0:T(4,128)(2,1)}, u32[]{:S(2)}) copy-start(bf16[4,1536]{1,0:T(4,128)(2,1)} %param.22) | copy-start | bytes 36868
  4.3 15.1 %copy-start.8 = (bf16[4,512]{1,0:T(4,128)(2,1)S(1)}, bf16[4,512]{1,0:T(4,128)(2,1)}, u32[]{:S(2)}) copy-start(bf16[4,512]{1,0:T(4,128)(2,1)} %param.23) | copy-start | bytes 12292
  4.3 15.1 %copy-start.9 = (bf16[4,512]{1,0:T(4,128)(2,1)S(1)}, bf16[4,512]{1,0:T(4,128)(2,1)}, u32[]{:S(2)}) copy-start(bf16[4,512]{1,0:T(4,128)(2,1)} %param.24) | copy-start | bytes 12292
  4.3 15.1 %copy-start.2 = (s32[128,8]{0,1:T(8,128)S(1)}, s32[128,8]{0,1:T(8,128)}, u32[]{:S(2)}) copy-start(s32[128,8]{0,1:T(8,128)} %param.34) | copy-start | bytes 12292
  4.3 15.2 %copy-start.10 = (f32[128,8]{0,1:T(8,128)S(1)}, f32[128,8]{0,1:T(8,128)}, u32[]{:S(2)}) copy-start(f32[128,8]{0,1:T(8,128)} %param.35) | copy-start | bytes 12292
  4.3 16.3 %copy-start.11 = (s32[4]{0:T(128)S(1)}, s32[4]{0:T(128)}, u32[]{:S(2)}) copy-start(s32[4]{0:T(128)} %param.26) | copy-start | bytes 52
  4.4 34.5 %all-to-all-start = ((bf16[32,176,128]{2,1,0:T(8,128)(2,1)}), bf16[32,176,128]{2,1,0:T(8,128)(2,1)S(1)}, u32[]{:S(2)}, u32[]{:S(2)}) async-start(bf16[32,176,128]{2,1,0:T(8,128)(2,1)} %pack.1), calls=%async_computation | async-start | bytes 2883584 | tf_op jit(solution)/shard_map/all_to_all | solution.py:397
  17.5 46.6 %collective-permute-start = (bf16[384,1536]{1,0:T(8,128)(2,1)}, bf16[384,1536]{1,0:T(8,128)(2,1)}, u32[]{:S(2)}, u32[]{:S(2)}) collective-permute-start(bf16[384,1536]{1,0:T(8,128)(2,1)} %pad_maximum_fusion), channel_id=1, source_target_pairs={{0,64},{32,96},{64,0},{96,32},{1,65},{33,97},{65,1},{97,33},{2,66}... | collective-permute-start | bytes 3538952 | tf_op jit(solution)/shard_map/ppermute | solution.py:462
  20.7 2.2 copy-start
  22.9 41.2 %copy-start.7 = (f32[1536]{0:T(1024)S(1)}, f32[1536]{0:T(1024)}, u32[]{:S(2)}) copy-start(f32[1536]{0:T(1024)} %param.30) | copy-start | bytes 18436
  22.9 53.1 %copy-start.1 = (bf16[128,1536]{1,0:T(8,128)(2,1)S(1)}, bf16[128,1536]{1,0:T(8,128)(2,1)}, u32[]{:S(2)}) copy-start(bf16[128,1536]{1,0:T(8,128)(2,1)} %resid_ref.1) | copy-start | bytes 1179652
  60.0 16.1 %all-to-all-start.1 = ((bf16[32,56,128]{2,1,0:T(8,128)(2,1)}), bf16[32,56,128]{2,1,0:T(8,128)(2,1)S(1)}, u32[]{:S(2)}, u32[]{:S(2)}) async-start(bf16[32,56,128]{2,1,0:T(8,128)(2,1)} %attention.1), calls=%async_computation.1 | async-start | bytes 917504 | tf_op jit(solution)/shard_map/all_to_all | solution.py:397
  82.6 55.8 %all-to-all-start.2 = ((bf16[32,40,1536]{2,1,0:T(8,128)(2,1)}), bf16[32,40,1536]{2,1,0:T(8,128)(2,1)}, u32[]{:S(2)}, u32[]{:S(2)}) async-start(bf16[32,40,1536]{2,1,0:T(8,128)(2,1)} %bitcast.32), calls=%async_computation.2 | async-start | bytes 7864320 | tf_op jit(solution)/shard_map/all_to_all | solution.py:397
  87.5 5.4 %collective-permute-start.1 = (bf16[384,1536]{1,0:T(8,128)(2,1)}, bf16[384,1536]{1,0:T(8,128)(2,1)S(1)}, u32[]{:S(2)}, u32[]{:S(2)}) collective-permute-start(bf16[384,1536]{1,0:T(8,128)(2,1)} %pad_maximum_fusion), channel_id=1, source_target_pairs={{0,32},{32,0},{64,96},{96,64},{1,33},{33,1},{65,97},{97,65},{2,34}... | collective-permute-start | bytes 3538952 | tf_op jit(solution)/shard_map/ppermute | solution.py:484
  87.6 8.8 %collective-permute-start.2 = (bf16[384,1536]{1,0:T(8,128)(2,1)}, bf16[384,1536]{1,0:T(8,128)(2,1)S(1)}, u32[]{:S(2)}, u32[]{:S(2)}) collective-permute-start(bf16[384,1536]{1,0:T(8,128)(2,1)} %collective-permute-done), channel_id=1, source_target_pairs={{0,32},{32,0},{64,96},{96,64},{1,33},{33,1},{65,97},{97,65},{2,34}... | collective-permute-start | bytes 3538952 | tf_op jit(solution)/shard_map/ppermute | solution.py:484
  149.4 67.7 %copy-start.6 = (bf16[4,1536]{1,0:T(4,128)(2,1)S(1)}, bf16[4,1536]{1,0:T(4,128)(2,1)}, u32[]{:S(2)}) copy-start(bf16[4,1536]{1,0:T(4,128)(2,1)} %param.25) | copy-start | bytes 36868
  149.4 71.4 %all-to-all-start.3 = ((bf16[32,40,1536]{2,1,0:T(8,128)(2,1)}), bf16[32,40,1536]{2,1,0:T(8,128)(2,1)}, u32[]{:S(2)}, u32[]{:S(2)}) async-start(bf16[32,40,1536]{2,1,0:T(8,128)(2,1)} %bitcast.31), calls=%async_computation.3 | async-start | bytes 7864320 | tf_op jit(solution)/shard_map/all_to_all | solution.py:397
  156.8 26.6 %collective-permute-start.3 = (bf16[1,8,128]{2,1,0:T(8,128)(2,1)S(1)}, bf16[1,8,128]{2,1,0:T(8,128)(2,1)S(1)}, u32[]{:S(2)}, u32[]{:S(2)}) collective-permute-start(bf16[1,8,128]{2,1,0:T(8,128)(2,1)S(1)} %pad_bitcast_fusion), channel_id=1, source_target_pairs={{0,1},{1,0},{2,3},{3,2},{4,5},{5,4},{6,7},{7,6},{8,9},{9,8},{10,11... | collective-permute-start | bytes 6152 | tf_op jit(solution)/shard_map/ppermute | solution.py:404
  183.4 16.4 %collective-permute-start.4 = (bf16[2,8,128]{2,1,0:T(8,128)(2,1)S(1)}, bf16[2,8,128]{2,1,0:T(8,128)(2,1)S(1)}, u32[]{:S(2)}, u32[]{:S(2)}) collective-permute-start(bf16[2,8,128]{2,1,0:T(8,128)(2,1)S(1)} %pad_maximum_fusion.5), channel_id=1, source_target_pairs={{0,2},{1,3},{2,0},{3,1},{4,6},{5,7},{6,4},{7,5},{8,10},{9,11},{10,... | collective-permute-start | bytes 12296 | tf_op jit(solution)/shard_map/ppermute | solution.py:404
  199.8 7.8 %collective-permute-start.5 = (bf16[4,8,128]{2,1,0:T(8,128)(2,1)S(1)}, bf16[4,8,128]{2,1,0:T(8,128)(2,1)S(1)}, u32[]{:S(2)}, u32[]{:S(2)}) collective-permute-start(bf16[4,8,128]{2,1,0:T(8,128)(2,1)S(1)} %pad_maximum_fusion.4), channel_id=1, source_target_pairs={{0,4},{1,5},{2,6},{3,7},{4,0},{5,1},{6,2},{7,3},{8,12},{9,13},{10,... | collective-permute-start | bytes 24584 | tf_op jit(solution)/shard_map/ppermute | solution.py:404
  207.6 3.8 %collective-permute-start.6 = (bf16[8,8,128]{2,1,0:T(8,128)(2,1)S(1)}, bf16[8,8,128]{2,1,0:T(8,128)(2,1)S(1)}, u32[]{:S(2)}, u32[]{:S(2)}) collective-permute-start(bf16[8,8,128]{2,1,0:T(8,128)(2,1)S(1)} %pad_maximum_fusion.3), channel_id=1, source_target_pairs={{0,8},{1,9},{2,10},{3,11},{4,12},{5,13},{6,14},{7,15},{8,0},{9,1},... | collective-permute-start | bytes 49160 | tf_op jit(solution)/shard_map/ppermute | solution.py:404
  211.4 5.5 %collective-permute-start.7 = (bf16[16,8,128]{2,1,0:T(8,128)(2,1)S(1)}, bf16[16,8,128]{2,1,0:T(8,128)(2,1)S(1)}, u32[]{:S(2)}, u32[]{:S(2)}) collective-permute-start(bf16[16,8,128]{2,1,0:T(8,128)(2,1)S(1)} %pad_maximum_fusion.2), channel_id=1, source_target_pairs={{0,16},{1,17},{2,18},{3,19},{4,20},{5,21},{6,22},{7,23},{8,24},{9,... | collective-permute-start | bytes 98312 | tf_op jit(solution)/shard_map/ppermute | solution.py:404
